TPU v7x, 256 devices: a whole 4x4x8 slice. The times are simulated.
256 devices in a mesh: seq: 32 (over z, x), fsdp: 8 (over y, core).
Axes of the slice: x: 4, y: 4, z: 8, core: 2. Of those that a mesh axis runs over, the one named last changes fastest.
Arguments:
- tokens: bfloat16 [24576, 6144], P('seq'), may hold values from -30 to 30
- w_query: bfloat16 [6144, 32, 128], P('seq', 'fsdp'), may hold values from -0.078125 to 0.078125
- w_keyval: bfloat16 [6144, 32, 256], P('seq', 'fsdp'), may hold values from -40 to 40
- doc_lengths: int32 [8], replicated, may hold values from 1 to 12288, 24576 in all
- norm_gain: bfloat16 [4096], P('fsdp'), may hold values from 0.25 to 1.75
Outputs:
- attended: bfloat16 [24576, 4096], P('seq', 'fsdp')
Inputs may be any that keep to these rules, and one draw needn't show every extreme that they name: `doc_lengths`: lengths are positive and sum to 24576; the longest document has exactly 12288 tokens.
All inputs are finite; a program needn't handle non-finite values.
Results may differ from a plain program's by a relative error of at most 0.0034.
Values may be sent and summed in bfloat16 or wider, within the bound.
A program may use at most 128 MiB of HBM per device.

v0:
```python
import jax
import jax.numpy as jnp
from jax import lax
from jax.sharding import PartitionSpec as P


def carried_in(value, axis, join, neutral):
    count, mine = (lax.axis_size(axis), lax.axis_index(axis))
    pieces = jax.tree.map(lambda part: lax.all_gather(part, axis), value)
    running = jax.tree.map(
        lambda part, zero: jnp.full_like(part, 0) + jnp.asarray(zero, part.dtype), value, neutral
    )

    def step(position, running):
        longer = join(running, jax.tree.map(lambda part: part[position], pieces))
        return jax.tree.map(lambda new, old: jnp.where(position < mine, new, old), longer, running)

    return lax.fori_loop(0, count - 1, step, running)


def doc_index(positions, doc_ends):
    return jnp.sum((positions[:, None] >= doc_ends[None, :]).astype(jnp.int32), axis=1)


def shards(tokens, w_query, w_keyval, doc_lengths, norm_gain):
    rows_here = tokens.shape[0]
    head_count = w_query.shape[1]
    head_size = w_query.shape[2]
    shard_index = lax.axis_index("seq")
    doc_ends = jnp.cumsum(doc_lengths)
    offsets = lax.iota(jnp.int32, rows_here)
    doc_ids = doc_index(shard_index * rows_here + offsets, doc_ends)
    first_doc = doc_ids[0]
    tail_doc = doc_ids[rows_here - 1]

    def project(panel_rows):
        panel = panel_rows.reshape(panel_rows.shape[0], panel_rows.shape[1] * panel_rows.shape[2])
        return jnp.dot(tokens, panel, preferred_element_type=jnp.float32)

    query_sum = project(lax.all_gather(w_query, "seq", axis=0, tiled=True))
    keyval_sum = project(lax.all_gather(w_keyval, "seq", axis=0, tiled=True))
    keyval = (
        jax.nn.silu(keyval_sum).astype(jnp.bfloat16).reshape(rows_here, head_count, 2 * head_size)
    )
    key_rows = keyval[:, :, :head_size]
    values = keyval[:, :, head_size:]
    tail_mask = (doc_ids == tail_doc).astype(jnp.bfloat16)
    tail_state = jnp.einsum(
        "thd,the->hde",
        key_rows * tail_mask[:, None, None],
        values,
        preferred_element_type=jnp.float32,
    )
    tail_begin = doc_ends[tail_doc] - doc_lengths[tail_doc]
    restart = (tail_begin >= shard_index * rows_here).astype(jnp.float32)

    def combine(earlier, newer):
        return (newer[0] + (1.0 - newer[1]) * earlier[0], jnp.maximum(earlier[1], newer[1]))

    incoming, _ = carried_in(
        (tail_state, restart),
        "seq",
        combine,
        (jnp.zeros_like(tail_state), jnp.zeros((), jnp.float32)),
    )
    before = doc_index(jnp.reshape(shard_index * rows_here - 1, (1,)), doc_ends)[0]
    incoming = incoming * (before == first_doc).astype(jnp.float32)
    queries = jax.nn.silu(query_sum).astype(jnp.bfloat16).reshape(rows_here, head_count, head_size)
    scores = jnp.einsum("thd,shd->hts", queries, key_rows, preferred_element_type=jnp.float32)
    causal = (
        (offsets[:, None] >= offsets[None, :]) & (doc_ids[:, None] == doc_ids[None, :])
    ).astype(jnp.float32)
    weights = (scores * causal[None]).astype(jnp.bfloat16)
    within = jnp.einsum("hts,she->the", weights, values, preferred_element_type=jnp.float32)
    carried = jnp.einsum(
        "thd,hde->the", queries, incoming.astype(jnp.bfloat16), preferred_element_type=jnp.float32
    )
    carried = carried * (doc_ids == first_doc).astype(jnp.float32)[:, None, None]
    mixed = within + carried
    sum_squares = lax.psum(jnp.sum(mixed * mixed, axis=(1, 2)), "fsdp")
    inverse_rms = lax.rsqrt(sum_squares / (head_count * lax.axis_size("fsdp") * head_size) + 1e-06)
    flat = mixed.reshape(rows_here, head_count * head_size)
    return (flat * inverse_rms[:, None] * norm_gain.astype(jnp.float32)[None, :]).astype(
        jnp.bfloat16
    )


def solution(mesh):
    return jax.shard_map(
        shards,
        mesh=mesh,
        in_specs=(P("seq", None), P("seq", "fsdp", None), P("seq", "fsdp", None), P(), P("fsdp")),
        out_specs=P("seq", "fsdp"),
        check_vma=False,
    )
```

profile of v0, /device:TPU:1, one launch (start us, length us, event | category | flops | bytes accessed | tf_op | source)
XLA Modules:
  0.0 427.5 jit_solution(9087954634818524678)
XLA Ops:
  9.6 1.2 compare_convert_fusion
  10.8 120.9 %all-gather.5.cloned.1.call-done = bf16[6144,4,256]{2,1,0:T(4,128)(2,1)} async-done(((bf16[192,4,256]{2,1,0:T(4,128)(2,1)}), bf16[6144,4,256]{2,1,0:T(4,128)(2,1)}) %all-gather.5.cloned.1.call-update) | async-done | bytes 12582928 | tf_op jit(solution)/shard_map/all_gather | solution.py:41
  131.7 9.3 %copy.33 = bf16[768,8,4,256]{3,1,2,0:T(8,128)(2,1)S(1)} copy(bf16[768,8,4,256]{3,2,1,0:T(4,128)(2,1)} %bitcast.40) | data formatting | bytes 25165824
  141.0 11.5 %multiply_convert_fusion.2 = bf16[768,1024]{1,0:T(8,128)(2,1)} fusion(bf16[768,6144]{1,0:T(8,128)(2,1)S(1)} %copy-done.2, bf16[6144,1024]{1,0:T(8,128)(2,1)S(1)} %bitcast.41), kind=kOutput, calls=%fused_computation.9 | convolution fusion | flops 9667608576 | bytes 23592960 | tf_op jit(solution)/shard_map/dot_general | solution.py:38
  152.5 2.9 reshape.105
  155.4 1.4 fusion.22
  156.9 1.9 copy.31
  158.7 1.3 fusion.13
  168.0 58.6 %all-reduce = f32[32]{0:T(128)S(1)} all-reduce(f32[32]{0:T(128)S(1)} %dynamic-update-slice), channel_id=1, replica_groups=mesh['seq'=32,'fsdp'=8] {'seq'}, use_global_device_ids=true, to_apply=%add | all-reduce | flops 32 | bytes 256
  226.9 11.6 %multiply_convert_fusion.4 = bf16[768,512]{0,1:T(8,128)(2,1)} fusion(bf16[768,6144]{1,0:T(8,128)(2,1)} %param.7, bf16[768,8,4,128]{3,2,1,0:T(4,128)(2,1)} %bitcast.47), kind=kOutput, calls=%fused_computation.17 | convolution fusion | flops 4833804288 | bytes 16515072 | tf_op jit(solution)/shard_map/dot_general | solution.py:38
  238.5 79.2 %all-gather.9.cloned.1.call-done = f32[128,128,128]{2,1,0:T(8,128)} async-done(((f32[4,128,128]{2,1,0:T(8,128)}), f32[128,128,128]{2,1,0:T(8,128)}) %all-gather.9.cloned.1.call-update) | async-done | bytes 8388624 | tf_op jit(solution)/shard_map/all_gather | solution.py:9
  317.7 78.4 %while.14 = (s32[]{:T(128)}, f32[4,128,128]{2,1,0:T(8,128)S(1)}, s32[]{:T(128)}, f32[32,4,128,128]{3,2,1,0:T(8,128)}, f32[32]{0:T(128)S(1)}, /*index=5*/s32[]{:T(128)}, f32[1]{0:T(128)}, s32[]{:T(128)}) while((s32[]{:T(128)}, f32[4,128,128]{2,1,0:T(8,128)S(1)}, s32[]{:T(128)}, f32[32,4,128,128]{3,2,1,0:T(8,128)}, f32[32]{0:T(128)S(1)}, ...), condition=%wide.region_3.4_spmd.clone, body=%wide.region_2.3_spmd.clone.sunk | while | flops 262149 | bytes 786569 | solution.py:18
  319.0 1.1 fusion.34
  321.6 1.1 fusion.34
  324.1 1.1 fusion.34
  326.6 1.1 fusion.34
  329.2 1.1 fusion.34
  331.7 1.1 fusion.34
  334.2 1.1 fusion.34
  336.7 1.1 fusion.34
  339.3 1.1 fusion.34
  341.8 1.1 fusion.34
  344.3 1.1 fusion.34
  346.9 1.1 fusion.34
  349.4 1.1 fusion.34
  351.9 1.1 fusion.34
  354.5 1.1 fusion.34
  357.0 1.1 fusion.34
  396.1 2.7 fusion.19
  398.8 6.0 %fusion.10 = (f32[768]{0:T(1024)S(1)}, f32[4,128,768]{2,1,0:T(8,128)}) fusion(f32[4,128,768]{2,1,0:T(8,128)} %fusion.19, f32[768]{0:T(1024)S(1)} %get-tuple-element.130, bf16[768,4,128]{0,2,1:T(8,128)(2,1)S(1)} %copy.31, f32[768,768]{1,0:T(8,128)S(1)} %fusion.9, bf16[768,4,128]{0,2,1:T(8,128)(2,1)} %bitcast.44, bf16[768,4,128]{2,1,0:T(4,128)(2,1)} %copy-done), kind=kOutput, calls=%fused_computation.14 | convolution fusion | flops 1214250240 | bytes 7870464 | tf_op jit(solution)/shard_map/hts,she->the/dot_general | solution.py:74
  404.8 1.9 copy.25
  406.7 13.2 %psum.7 = f32[768]{0:T(1024)S(1)} all-reduce(f32[768]{0:T(1024)S(1)} %get-tuple-element.134), channel_id=1, replica_groups=mesh['seq'=32,'fsdp'=8] {'fsdp'}, use_global_device_ids=true, to_apply=%region_6.7 | all-reduce | flops 768 | bytes 6144 | tf_op jit(solution)/shard_map/psum | solution.py:80
  (78 shorter events, 45.6 us)
Async XLA Ops:
  6.5 125.1 %all-gather.5.cloned.1.call-start = ((), (), s32[]{:S(2)}) async-start(), calls=%async_computation | async-start | bytes 12976128 | tf_op jit(solution)/shard_map/all_gather | solution.py:41
  7.3 219.6 %all-gather.7.cloned.1.call-start = ((), (), s32[]{:S(2)}) async-start(), calls=%async_computation.1 | async-start | bytes 6488064 | tf_op jit(solution)/shard_map/all_gather | solution.py:40
  8.0 309.7 %all-gather.9.cloned.1.call-start = ((), (), s32[]{:S(2)}) async-start(), calls=%async_computation.2 | async-start | bytes 8650752 | tf_op jit(solution)/shard_map/all_gather | solution.py:9
  131.7 9.3 %copy-start.2 = (bf16[768,6144]{1,0:T(8,128)(2,1)S(1)}, bf16[768,6144]{1,0:T(8,128)(2,1)}, u32[]{:S(2)}) copy-start(bf16[768,6144]{1,0:T(8,128)(2,1)} %param.7) | copy-start | bytes 28311556
  156.9 11.1 %copy-start = (bf16[768,4,128]{2,1,0:T(4,128)(2,1)}, bf16[768,4,128]{2,1,0:T(4,128)(2,1)S(1)}, u32[]{:S(2)}) copy-start(bf16[768,4,128]{2,1,0:T(4,128)(2,1)S(1)} %get-tuple-element.128) | copy-start | bytes 2359300
  156.9 5.6 %copy-start.3 = (s32[8]{0:T(128)S(1)}, s32[8]{0:T(128)}, u32[]{:S(2)}) copy-start(s32[8]{0:T(128)} %param.10) | copy-start | bytes 100
  156.9 9.6 %copy-start.1 = (bf16[512]{0:T(512)(128)(2,1)S(1)}, bf16[512]{0:T(512)(128)(2,1)}, u32[]{:S(2)}) copy-start(bf16[512]{0:T(512)(128)(2,1)} %param.11) | copy-start | bytes 3076
  156.9 9.6 %copy-start.4 = (u32[256]{0:T(256)S(1)}, u32[256]{0:T(256)}, u32[]{:S(2)}) copy-start(u32[256]{0:T(256)} %constant.65) | copy-start | bytes 3076
Sparse Core Ops, SparseCore 0:
  9.9 121.7 all-gather.4
  134.3 85.5 all-gather.6
  222.5 95.1 all-gather.8
where the time goes:
time: 429 us; the launch traced here: 427 us
  waiting for transfers between devices  201 us (47%)
  blocking collectives  71.8 us (17%)
  local copies, waits for them, and re-layouts  41.2 us (10%)
  other arithmetic  39.8 us (9%)
  matrix products  33.1 us (8%)
  loops' own time  22.3 us (5%)
  between operations  17.7 us (4%)
    all_gather x1, waiting for transfers between devices, shards(): keyval_sum = project(lax.all_gather(w_keyval, 'seq', axis=0, tiled=True))  121 us
    all_gather x1, waiting for transfers between devices, carried_in(): pieces = jax.tree.map(lambda part: lax.all_gather(part, axis), value)  79.2 us
    unnamed x1, blocking collectives  58.6 us
    select_n x31, other arithmetic, step(): jnp.where(position < mine, new, old)  35.6 us
    dot_general x2, matrix products, project(): return jnp.dot(tokens, panel, preferred_element_type=jnp.float32)  23.1 us
    another operation x1, loops' own time, carried_in(): return lax.fori_loop(0, count - 1, step, running)  22.3 us
    dynamic_slice x31, local copies, waits for them, and re-layouts, step(): longer = join(running, jax.tree.map(lambda part: part[position], pieces))  20.6 us
    psum x1, blocking collectives, shards(): sum_squares = lax.psum(jnp.sum(mixed * mixed, axis=(1, 2)), 'fsdp')  13.2 us
  transfers between devices with their start and end apart: 3, of which 2 were waited for; matrix products, arithmetic and copies ran while one was open for 11% of the time, Pallas kernels for 0%

commit v1 on v0

v1 whole, which is shorter than its diff:
```python
import functools

import jax
import jax.numpy as jnp
from jax import lax
from jax.experimental import pallas as pl
from jax.experimental.pallas import tpu as pltpu
from jax.sharding import Mesh, PartitionSpec as P

NZ, NX, NY, NC = 8, 4, 4, 2
UNITS = 6
ROWS = 192
PR = 80
QR = ROWS - PR
WID = 256
TOK = 768
DM = 6144
DH = 128
HEADS = 4
MESH = pl.DeviceIdType.MESH


def doc_ends(len_ref):
    ends, total = [], jnp.int32(0)
    for i in range(8):
        total = total + len_ref[i]
        ends.append(total)
    return ends


def start_of(position, ends):
    start = jnp.zeros_like(position)
    for end in ends:
        start = jnp.maximum(start, jnp.where(position >= end, end, 0))
    return start


def gather_kernel(
    len_ref, tok_hbm, w_hbm, qkv_ref, tails_ref,
    wbuf, tokv, acc, local_sem,
    px_s, px_r, qz_s, qz_r, pz_s, pz_r, qx_s, qx_r,
):
    mz, mx = lax.axis_index("z"), lax.axis_index("x")
    shard = mz * NX + mx
    ends = doc_ends(len_ref)

    own = pltpu.make_async_copy(w_hbm, wbuf.at[:, mz, mx], local_sem.at[0])
    own.start()
    tok_copy = pltpu.make_async_copy(tok_hbm, tokv, local_sem.at[1])
    tok_copy.start()

    def z_at(delta):
        return lax.rem(mz + delta + NZ, NZ)

    def x_at(delta):
        return lax.rem(mx + delta + NX, NX)

    barrier = pltpu.get_barrier_semaphore()
    for delta in (1, -1):
        pl.semaphore_signal(barrier, inc=1, device_id={"z": z_at(delta)}, device_id_type=MESH)
        pl.semaphore_signal(barrier, inc=1, device_id={"x": x_at(delta)}, device_id_type=MESH)
    pl.semaphore_wait(barrier, 4)
    own.wait()

    def copy(ref, send, recv, target):
        return pltpu.make_async_remote_copy(
            src_ref=ref, dst_ref=ref, send_sem=send, recv_sem=recv,
            device_id=target, device_id_type=MESH,
        )

    def px(u, d, s, lag):
        sign = 1 - 2 * d
        block = x_at(-sign * (s + lag))
        rows = (0, PR) if s == 0 else ((0, 48) if d == 0 else (48, 32))
        return copy(
            wbuf.at[u, mz, block, pl.ds(*rows), :], px_s.at[u, d, s], px_r.at[u, d, s],
            {"x": x_at(sign)},
        )

    def qz(u, d, s, lag):
        sign = 1 - 2 * d
        block = z_at(-sign * (s + lag))
        rows = (PR, QR) if s < 3 else ((PR, 48) if d == 0 else (PR + 48, QR - 48))
        return copy(
            wbuf.at[u, block, mx, pl.ds(*rows), :], qz_s.at[u, d, s], qz_r.at[u, d, s],
            {"z": z_at(sign)},
        )

    def pz(u, d, s, c, lag):
        sign = 1 - 2 * d
        block = z_at(-sign * (s + lag))
        return copy(
            wbuf.at[u, block, pl.ds(2 * c, 2), pl.ds(0, PR), :],
            pz_s.at[u, d, s, c], pz_r.at[u, d, s, c], {"z": z_at(sign)},
        )

    def qx(u, d, s, c, lag):
        sign = 1 - 2 * d
        block = x_at(-sign * (s + lag))
        return copy(
            wbuf.at[u, pl.ds(2 * c, 2), block, pl.ds(PR, QR), :],
            qx_s.at[u, d, s, c], qx_r.at[u, d, s, c], {"x": x_at(sign)},
        )

    qx_order = ((0, 1, 2, 3), (2, 3, 0, 1))

    def round_body(r, carry):
        n, p, c = r, r - 1, r - 2
        first, second, third = r < UNITS, (r >= 1) & (r <= UNITS), r >= 2

        def compute(step):
            lo = step * (DM // 4)
            part = jnp.dot(
                tokv[:, lo:lo + DM // 4],
                wbuf[c, 2 * step:2 * step + 2].reshape(DM // 4, WID),
                preferred_element_type=jnp.float32,
            )
            if step == 0:
                acc[...] = part
            else:
                acc[...] += part

        @pl.when(first)
        def _():
            for d in (0, 1):
                qz(n, d, 0, 0).start()
                px(n, d, 0, 0).start()

        @pl.when(second)
        def _():
            for d in (0, 1):
                px(p, d, 1, 1).wait_recv()
            for k in (0, 1):
                for d in (0, 1):
                    pz(p, d, 0, k, 0).start()
            for d in (0, 1):
                qz(p, d, 3, 1).wait_recv()
            for k in range(4):
                for d in (0, 1):
                    qx(p, d, 0, qx_order[d][k], 0).start()

        @pl.when(third)
        def _():
            pz(c, 0, 3, 0, 1).wait_recv()
            pz(c, 1, 3, 1, 1).wait_recv()
            for d in (0, 1):
                for k in (2, 3):
                    qx(c, d, 0, qx_order[d][k], 1).wait_recv()
                for k in (0, 1):
                    qx(c, d, 1, qx_order[d][k], 1).wait_recv()

        @pl.when(r == 2)
        def _():
            tok_copy.wait()

        @pl.when(third)
        def _():
            compute(0)

        for s in (1, 2, 3):
            @pl.when(first)
            def _():
                for d in (0, 1):
                    qz(n, d, s - 1, 1).wait_recv()
                    qz(n, d, s, 0).start()
                    if s == 1:
                        px(n, d, 0, 1).wait_recv()
                if s == 1:
                    for d in (0, 1):
                        px(n, d, 1, 0).start()

            @pl.when(second)
            def _():
                for k in (0, 1):
                    for d in (0, 1):
                        pz(p, d, s - 1, k, 1).wait_recv()
                        if s < 3 or k == d:
                            pz(p, d, s, k, 0).start()
                if s < 3:
                    for d in (0, 1):
                        qx(p, d, 0, qx_order[d][s - 1], 1).wait_recv()
                        qx(p, d, 1, qx_order[d][s - 1], 0).start()

            @pl.when(third)
            def _():
                compute(s)

        @pl.when(third)
        def _():
            total = acc[...]
            act = (total / (1.0 + jnp.exp(-total))).astype(jnp.bfloat16)
            qkv_ref[c] = act

            @pl.when(c < HEADS)
            def _():
                position = lax.broadcasted_iota(jnp.int32, (TOK, DH), 0) + shard * TOK
                last = start_of(shard * TOK + TOK - 1, ends)
                keys = act[:, :DH]
                kept = jnp.where(position >= last, keys, jnp.zeros_like(keys))
                tails_ref[c] = lax.dot_general(
                    kept, act[:, DH:], (((0,), (0,)), ((), ())),
                    preferred_element_type=jnp.float32,
                )

        return carry

    lax.fori_loop(0, UNITS + 2, round_body, 0)

    def drain(u, carry):
        for d in (0, 1):
            for s in (0, 1):
                px(u, d, s, 0).wait_send()
            for s in range(4):
                qz(u, d, s, 0).wait_send()
                for k in (0, 1):
                    if s < 3 or k == d:
                        pz(u, d, s, k, 0).wait_send()
            for k in range(4):
                qx(u, d, 0, qx_order[d][k], 0).wait_send()
                if k < 2:
                    qx(u, d, 1, qx_order[d][k], 0).wait_send()
        return carry

    lax.fori_loop(0, UNITS, drain, 0)


def attend_kernel(
    len_ref, qkv_ref, tails_ref, gain_ref, out_ref,
    t4, rt, inc_send, inc_recv, mixed, sums, inv_ref,
    ta_s, ta_r, rt_s, rt_r, ia_s, ia_r, sq_s, sq_r,
):
    mz, mx = lax.axis_index("z"), lax.axis_index("x")
    me = lax.axis_index("y") * NC + lax.axis_index("core")
    shard = mz * NX + mx
    ends = doc_ends(len_ref)

    def x_at(delta):
        return lax.rem(mx + delta + NX, NX)

    def z_at(delta):
        return lax.rem(mz + delta + NZ, NZ)

    def peer(delta):
        index = lax.rem(me + delta, NY * NC)
        return {"y": index // NC, "core": lax.rem(index, NC)}

    barrier = pltpu.get_barrier_semaphore()
    for k in range(1, NX):
        pl.semaphore_signal(barrier, inc=1, device_id={"x": x_at(k)}, device_id_type=MESH)
    for delta in (1, -1):
        pl.semaphore_signal(barrier, inc=1, device_id={"z": z_at(delta)}, device_id_type=MESH)
    for k in range(1, NY * NC):
        pl.semaphore_signal(barrier, inc=1, device_id=peer(k), device_id_type=MESH)
    pl.semaphore_wait(barrier, NX - 1 + 2 + NY * NC - 1)

    def copy(src, dst, send, recv, target):
        return pltpu.make_async_remote_copy(
            src_ref=src, dst_ref=dst, send_sem=send, recv_sem=recv,
            device_id=target, device_id_type=MESH,
        )

    def tail_to(k):
        return copy(tails_ref.at[x_at(k)], t4.at[mx], ta_s.at[k], ta_r.at[k], {"x": x_at(k)})

    def tail_from(k):
        return copy(tails_ref.at[mx], t4.at[x_at(-k)], ta_s.at[k], ta_r.at[k], {"x": x_at(k)})

    def relay(s):
        return copy(rt.at[s], rt.at[s + 1], rt_s.at[s], rt_r.at[s], {"z": z_at(1)})

    def inc_to(k):
        return copy(
            inc_send.at[x_at(k)], inc_recv.at[mx], ia_s.at[k], ia_r.at[k], {"x": x_at(k)}
        )

    def inc_from(k):
        return copy(
            inc_send.at[mx], inc_recv.at[x_at(-k)], ia_s.at[k], ia_r.at[k], {"x": x_at(k)}
        )

    def square_to(k):
        return copy(sums.at[0], sums.at[k], sq_s.at[k], sq_r.at[k], peer(k))

    for k in range(1, NX):
        tail_to(k).start()
    t4[mx] = tails_ref[mx]

    tile = 256
    base = shard * TOK

    def within(h):
        pos = h // 2
        off = (h % 2) * DH
        for i in range(TOK // tile):
            width = (i + 1) * tile
            q = qkv_ref[4 + pos, i * tile:(i + 1) * tile, off:off + DH]
            k = qkv_ref[h, 0:width, 0:DH]
            v = qkv_ref[h, 0:width, DH:2 * DH]
            scores = lax.dot_general(
                q, k, (((1,), (1,)), ((), ())), preferred_element_type=jnp.float32
            )
            t = lax.broadcasted_iota(jnp.int32, (tile, 1), 0) + (base + i * tile)
            begin = start_of(t, ends)
            s = lax.broadcasted_iota(jnp.int32, (1, width), 1) + base
            keep = (s <= t) & (s >= begin)
            weights = jnp.where(keep, scores, 0.0).astype(jnp.bfloat16)
            mixed[i * tile:(i + 1) * tile, h * DH:(h + 1) * DH] = jnp.dot(
                weights, v, preferred_element_type=jnp.float32
            )

    within(0)
    for k in range(1, NX):
        tail_from(k).wait_recv()
    row_last = start_of((mz + 1) * (NX * TOK) - 1, ends)
    total = jnp.zeros((DH, DH), jnp.float32)
    for j in range(NX):
        here = ((mz * NX + j + 1) * TOK - 1 >= row_last).astype(jnp.float32)
        total = total + here * t4[j]
    rt[0] = total
    within(1)
    relay(0).start()
    for s in (1, 2, 3):
        if s < 3:
            within(s + 1)
        relay(s - 1).wait_recv()
        relay(s).start()
    relay(3).wait_recv()

    row_first = start_of(mz * (NX * TOK), ends)
    before = jnp.zeros((DH, DH), jnp.float32)
    for d in range(1, 5):
        row = mz - d
        used = (row >= 0) & ((row + 1) * (NX * TOK) - 1 >= row_first)
        before = before + used.astype(jnp.float32) * rt[d]
    for j in range(NX):
        begin = start_of((mz * NX + j) * TOK, ends)
        state = (begin <= mz * (NX * TOK) - 1).astype(jnp.float32) * before
        for i in range(j):
            used = ((mz * NX + i + 1) * TOK - 1 >= begin).astype(jnp.float32)
            state = state + used * t4[i]
        inc_send[j] = state.astype(jnp.bfloat16)
    for k in range(1, NX):
        inc_to(k).start()
    inc_recv[mx] = inc_send[mx]
    for k in range(1, NX):
        inc_from(k).wait_recv()

    t = lax.broadcasted_iota(jnp.int32, (TOK, 1), 0) + base
    carried_on = (start_of(t, ends) <= base).astype(jnp.float32)
    squares = jnp.zeros((TOK, DH), jnp.float32)
    for h in range(HEADS):
        off = (h % 2) * DH
        q = qkv_ref[4 + h // 2, :, off:off + DH]
        carried = jnp.dot(q, inc_recv[h], preferred_element_type=jnp.float32)
        value = mixed[:, h * DH:(h + 1) * DH] + carried * carried_on
        mixed[:, h * DH:(h + 1) * DH] = value
        squares = squares + value * value
    for i in range(TOK // DH):
        flipped = squares[i * DH:(i + 1) * DH, :].T
        sums[0, i:i + 1, :] = jnp.sum(flipped, axis=0, keepdims=True)
    sums[0, 6:8, :] = jnp.zeros((2, DH), jnp.float32)
    for k in range(1, NY * NC):
        square_to(k).start()
    for k in range(1, NY * NC):
        square_to(k).wait_recv()
    total = sums[0]
    for k in range(1, NY * NC):
        total = total + sums[k]
    inv_ref[...] = lax.rsqrt(total / (HEADS * NY * NC * DH) + 1e-06)
    gain = gain_ref[...].astype(jnp.float32)
    for i in range(TOK // DH):
        scale = jnp.broadcast_to(inv_ref[i:i + 1, :], (DH, DH)).T
        for h in range(HEADS):
            value = mixed[i * DH:(i + 1) * DH, h * DH:(h + 1) * DH]
            out_ref[i * DH:(i + 1) * DH, h * DH:(h + 1) * DH] = (
                value * scale * gain[:, h * DH:(h + 1) * DH]
            ).astype(jnp.bfloat16)

    for k in range(1, NX):
        tail_to(k).wait_send()
        inc_to(k).wait_send()
    for s in range(4):
        relay(s).wait_send()
    for k in range(1, NY * NC):
        square_to(k).wait_send()


def shards(tokens, w_query, w_keyval, doc_lengths, norm_gain):
    units = [w_keyval[:, h, :] for h in range(HEADS)]
    units += [w_query[:, 2 * j:2 * j + 2, :].reshape(ROWS, WID) for j in range(2)]
    w_in = jnp.stack(units)
    dma = pltpu.SemaphoreType.DMA
    vmem = pl.BlockSpec(memory_space=pltpu.VMEM)
    smem = pl.BlockSpec(memory_space=pltpu.SMEM)
    anywhere = pl.BlockSpec(memory_space=pl.ANY)
    qkv, tails = pl.pallas_call(
        gather_kernel,
        out_shape=(
            jax.ShapeDtypeStruct((UNITS, TOK, WID), jnp.bfloat16),
            jax.ShapeDtypeStruct((HEADS, DH, DH), jnp.float32),
        ),
        in_specs=[smem, anywhere, anywhere],
        out_specs=(vmem, vmem),
        scratch_shapes=[
            pltpu.VMEM((UNITS, NZ, NX, ROWS, WID), jnp.bfloat16),
            pltpu.VMEM((TOK, DM), jnp.bfloat16),
            pltpu.VMEM((TOK, WID), jnp.float32),
            dma((2,)),
            dma((UNITS, 2, 2)), dma((UNITS, 2, 2)),
            dma((UNITS, 2, 4)), dma((UNITS, 2, 4)),
            dma((UNITS, 2, 4, 2)), dma((UNITS, 2, 4, 2)),
            dma((UNITS, 2, 2, 4)), dma((UNITS, 2, 2, 4)),
        ],
        compiler_params=pltpu.CompilerParams(
            collective_id=0, has_side_effects=True, vmem_limit_bytes=60 << 20
        ),
        name="gather",
    )(doc_lengths, tokens, w_in)
    peers = NY * NC
    return pl.pallas_call(
        attend_kernel,
        out_shape=jax.ShapeDtypeStruct((TOK, HEADS * DH), jnp.bfloat16),
        in_specs=[smem, vmem, vmem, vmem],
        out_specs=vmem,
        scratch_shapes=[
            pltpu.VMEM((NX, DH, DH), jnp.float32),
            pltpu.VMEM((5, DH, DH), jnp.float32),
            pltpu.VMEM((NX, DH, DH), jnp.bfloat16),
            pltpu.VMEM((NX, DH, DH), jnp.bfloat16),
            pltpu.VMEM((TOK, HEADS * DH), jnp.float32),
            pltpu.VMEM((peers, 8, DH), jnp.float32),
            pltpu.VMEM((8, DH), jnp.float32),
            dma((NX,)), dma((NX,)), dma((4,)), dma((4,)),
            dma((NX,)), dma((NX,)), dma((peers,)), dma((peers,)),
        ],
        compiler_params=pltpu.CompilerParams(
            collective_id=1, has_side_effects=True, vmem_limit_bytes=60 << 20
        ),
        name="attend",
    )(doc_lengths, qkv, tails, norm_gain.reshape(1, HEADS * DH))


def solution(mesh):
    grid = Mesh(mesh.devices.reshape(NZ, NX, NY, NC), ("z", "x", "y", "core"))
    seq, fsdp = ("z", "x"), ("y", "core")
    return jax.shard_map(
        shards,
        mesh=grid,
        in_specs=(P(seq, None), P(seq, fsdp, None), P(seq, fsdp, None), P(), P(fsdp)),
        out_specs=P(seq, fsdp),
        check_vma=False,
    )
```

time: 429 us -> 179 us (0.42)
  waiting for transfers between devices: 201 us -> 0 us
  Pallas kernels: 0 us -> 171 us
  blocking collectives: 71.8 us -> 0 us
  other arithmetic: 39.8 us -> 0 us
  local copies, waits for them, and re-layouts: 41.2 us -> 7.86 us
  matrix products: 33.1 us -> 0 us
  loops' own time: 22.3 us -> 0 us
  between operations: 17.7 us -> 0.09 us
    all_gather x3 -> x0, waiting for transfers between devices: 200 us -> none  [the longest x1 121 us: shards(): keyval_sum = project(lax.all_gather(w_keyval, 'seq', axis=0, tiled=True))]
    pallas_call x0 -> x2, Pallas kernels: none -> 171 us  [the longest x1 125 us: shards(): pl.pallas_call(gather_kernel, out_shape=(jax.ShapeDtypeStruct((UNITS, TOK...]
    unnamed x1 -> x0, blocking collectives: 58.6 us -> none
    select_n x31 -> x0, other arithmetic: 35.6 us -> none  [step(): jnp.where(position < mine, new, old)]
    dot_general x5 -> x0, matrix products: 33.1 us -> none  [the longest x2 23.1 us: project(): return jnp.dot(tokens, panel, preferred_element_type=jnp.float32)]
    another operation x1 -> x0, loops' own time: 22.3 us -> none  [carried_in(): return lax.fori_loop(0, count - 1, step, running)]
    dynamic_slice x33 -> x0, local copies, waits for them, and re-layouts: 21.8 us -> none  [the longest x31 20.6 us: step(): longer = join(running, jax.tree.map(lambda part: part[position], pieces))]
    psum x1 -> x0, blocking collectives: 13.2 us -> none  [shards(): sum_squares = lax.psum(jnp.sum(mixed * mixed, axis=(1, 2)), 'fsdp')]
  transfers between devices with their start and end apart: 3 -> 0, of which waited for: 2 -> 0; matrix products, arithmetic and copies ran while one was open for 11% -> 0% of each run, Pallas kernels for 0% -> 0%
where the time goes in v1:
time: 179 us
  Pallas kernels  171 us (96%)
  local copies, waits for them, and re-layouts  7.86 us (4%)
    pallas_call x1, Pallas kernels, shards(): pl.pallas_call(gather_kernel, out_shape=(jax.ShapeDtypeStruct((UNITS, TOK...  125 us
    pallas_call x1, Pallas kernels, shards(): pl.pallas_call(attend_kernel, out_shape=jax.ShapeDtypeStruct((TOK, HEADS...  45.5 us

profile of v1, /device:TPU:1, one launch (start us, length us, event | category | flops | bytes accessed | tf_op | source)
XLA Modules:
  0.0 178.7 jit_solution(15316364893835022984)
XLA Ops:
  0.0 1.3 reshape.3.gain_ref
  1.3 1.2 fusion.5
  2.5 0.1 stack_reshape.7
  2.5 0.1 stack_reshape.6
  2.6 2.3 %fusion.4 = (bf16[192,1,256]{2,1,0:T(2,128)(2,1)S(1)}, bf16[192,1,256]{2,1,0:T(2,128)(2,1)S(1)}, bf16[192,1,256]{2,1,0:T(2,128)(2,1)S(1)}, bf16[192,1,256]{2,1,0:T(2,128)(2,1)S(1)}) fusion(bf16[192,4,256]{2,1,0:T(4,128)(2,1)} %param.7), kind=kLoop, calls=%fused_computation.10 | loop fusion | bytes 786432 | tf_op jit(solution)/shard_map/slice | solution.py:389
  5.1 0.0 copy-start
  5.1 0.8 copy-done
  5.9 125.3 %gather.1 = (bf16[6,768,256]{2,1,0:T(8,128)(2,1)}, f32[4,128,128]{2,1,0:T(8,128)}) custom-call(s32[8]{0:T(128)} %len_ref.3, bf16[768,6144]{1,0:T(8,128)(2,1)} %tok_hbm.1, bf16[6,192,256]{2,1,0:T(8,128)(2,1)} %copy-done), custom_call_target="tpu_custom_call" | custom-call | tf_op jit(solution)/shard_map/gather/pallas_call | solution.py:396
  131.2 45.5 %attend.1 = bf16[768,512]{1,0:T(8,128)(2,1)} custom-call(s32[8]{0:T(128)} %len_ref.3, bf16[6,768,256]{2,1,0:T(8,128)(2,1)} %get-tuple-element.7.qkv_ref, f32[4,128,128]{2,1,0:T(8,128)} %get-tuple-element.8.tails_ref, bf16[1,512]{1,0:T(2,128)(2,1)} %reshape.3.gain_ref), custom_call_target="tpu_custom_call" | custom-call | tf_op jit(solution)/shard_map/attend/pallas_call | solution.py:420
  176.7 2.1 %copy.36 = bf16[768,512]{1,0:T(8,128)(2,1)} copy(bf16[768,512]{1,0:T(8,128)(2,1)} %attend.1) | data formatting | bytes 1572864
  (6 shorter events, 0.1 us)
Async XLA Ops:
  5.1 0.8 copy-start

commit v2 on v0

v2 whole, which is shorter than its diff:
```python
import jax
import jax.numpy as jnp
from jax import lax
from jax.experimental import pallas as pl
from jax.experimental.pallas import tpu as pltpu
from jax.sharding import Mesh, PartitionSpec as P

NZ, NX, NY, NC = 8, 4, 4, 2
PEERS = NY * NC
UNITS = 3
ROWS = 192
PR = 80
QR = ROWS - PR
WID = 256
TOK = 768
DM = 6144
DH = 128
PIECE = TOK // PEERS
SUB = PIECE // 3
TILE = 256
TILES = TOK // TILE
MESH = pl.DeviceIdType.MESH


def doc_ends(len_ref):
    ends, total = [], jnp.int32(0)
    for i in range(8):
        total = total + len_ref[i]
        ends.append(total)
    return ends


def start_of(position, ends):
    start = jnp.zeros_like(position)
    for end in ends:
        start = jnp.maximum(start, jnp.where(position >= end, end, 0))
    return start


def kernel(
    len_ref, tok_hbm, w_hbm, gain_ref, out_ref,
    wbuf, tbuf, tpb, tokv, acc, qkv, starts, tails, t4, rt, inc_send, inc,
    mixed, sums, osend, orecv, local_sem,
    pxm, pxp, pxf, qzm, qzt, pz, qxm, qxp, qxf, t1, t2, t3,
    ta, rl, ia, sq, oe,
):
    mz, mx = lax.axis_index("z"), lax.axis_index("x")
    my, mc = lax.axis_index("y"), lax.axis_index("core")
    me = my * NC + mc
    mate = mx + 1 - 2 * lax.rem(mx, 2)
    partner = NX - 1 - mx
    across = NX - 1 - mate
    group = mx // 2
    mine = lax.rem(mx, 2)
    ends = doc_ends(len_ref)
    blocks = (mz * NX + mx, mz * NX + partner)
    bases = (blocks[0] * TOK, blocks[1] * TOK)

    stage = (
        pltpu.make_async_copy(w_hbm.at[group], wbuf.at[:, mz, mx], local_sem.at[0]),
        pltpu.make_async_copy(
            w_hbm.at[1 - group, :, pl.ds(PR, QR), :], tbuf.at[:, mz], local_sem.at[1]
        ),
        pltpu.make_async_copy(w_hbm.at[1 - group, :, pl.ds(0, PR), :], tpb, local_sem.at[2]),
    )
    for item in stage:
        item.start()
    tok_copy = pltpu.make_async_copy(tok_hbm, tokv.at[0], local_sem.at[3])
    tok_copy.start()

    def z_at(delta):
        return lax.rem(mz + delta + NZ, NZ)

    def y_at(delta):
        return lax.rem(my + delta + NY, NY)

    def peer(side, k):
        index = lax.rem(me + k, PEERS)
        return {
            "x": mx if side == 0 else partner,
            "y": index // NC,
            "core": lax.rem(index, NC),
        }

    barrier = pltpu.get_barrier_semaphore()

    def greet(target):
        pl.semaphore_signal(barrier, inc=1, device_id=target, device_id_type=MESH)

    greet({"x": mate})
    greet({"z": z_at(1)})
    greet({"z": z_at(-1)})
    for k in range(PEERS):
        if k:
            greet(peer(0, k))
        greet(peer(1, k))
    pl.semaphore_wait(barrier, 3 + 2 * PEERS - 1)
    for item in stage:
        item.wait()

    def copy(src, dst, sems, index, target):
        return pltpu.make_async_remote_copy(
            src_ref=src, dst_ref=dst, send_sem=sems.at[(0, *index)],
            recv_sem=sems.at[(1, *index)], device_id=target, device_id_type=MESH,
        )

    def same(ref, sems, index, target):
        return copy(ref, ref, sems, index, target)

    to_mate, to_partner = {"x": mate}, {"x": partner}

    def upper(u, x):
        return wbuf.at[u, mz, x, pl.ds(0, PR), :]

    def px_mate(u, x):
        return same(upper(u, x), pxm, (u,), to_mate)

    def px_partner(u, x):
        return copy(tpb.at[u], upper(u, x), pxp, (u,), to_partner)

    def px_forward(u, x):
        return same(upper(u, x), pxf, (u,), to_mate)

    def qz(u, d, s, lag):
        sign = 1 - 2 * d
        block = z_at(-sign * (s + lag))
        lo, size = (0, QR) if s < 3 else ((0, 48) if d == 0 else (48, QR - 48))
        target = {"z": z_at(sign)}
        return (
            same(wbuf.at[u, block, mx, pl.ds(PR + lo, size), :], qzm, (u, d, s), target),
            same(tbuf.at[u, block, pl.ds(lo, size), :], qzt, (u, d, s), target),
        )

    def pzc(u, d, s, k, lag):
        sign = 1 - 2 * d
        block = z_at(-sign * (s + lag))
        return same(
            wbuf.at[u, block, pl.ds(2 * k, 2), pl.ds(0, PR), :],
            pz, (u, d, s, k), {"z": z_at(sign)},
        )

    def lower(u, k, x):
        return wbuf.at[u, pl.ds(2 * k, 2), x, pl.ds(PR, QR), :]

    def qx_mate(u, k, x):
        return same(lower(u, k, x), qxm, (u, k), to_mate)

    def qx_partner(u, k, x):
        return copy(tbuf.at[u, pl.ds(2 * k, 2)], lower(u, k, x), qxp, (u, k), to_partner)

    def qx_forward(u, k, x):
        return same(lower(u, k, x), qxf, (u, k), to_mate)

    def token_rows(y, core, j, half=None):
        start = (y * NC + core) * PIECE + j * SUB
        if half is None:
            return tokv.at[1, pl.ds(start, SUB), :]
        return tokv.at[1, pl.ds(start + half * (SUB // 2), SUB // 2), :]

    def tok_x(j):
        start = me * PIECE + j * SUB
        return copy(tok_hbm.at[pl.ds(start, SUB), :], token_rows(my, mc, j), t1, (j,), to_partner)

    def tok_y(j, d, s, lag):
        sign = 1 - 2 * d
        rows = token_rows(y_at(-sign * (s + lag)), mc, j, None if s == 0 else d)
        return same(rows, t2, (j, d, s), {"y": y_at(sign)})

    def tok_core(j, delta, receive):
        core = 1 - mc if receive else mc
        return same(token_rows(y_at(delta), core, j), t3, (j, delta % NY), {"core": 1 - mc})

    def tokens_in(j):
        tok_x(j).wait_recv()
        for d in (0, 1):
            tok_y(j, d, 0, 0).start()
        tok_core(j, 0, False).start()

    def tokens_hop(j):
        for d in (0, 1):
            tok_y(j, d, 0, 1).wait_recv()
            tok_y(j, d, 1, 0).start()
        for delta in (1, -1):
            tok_core(j, delta, False).start()

    def tokens_last(j):
        for d in (0, 1):
            tok_y(j, d, 1, 1).wait_recv()
        tok_core(j, 2, False).start()

    def tokens_end():
        for j in range(3):
            for delta in (0, 1, -1, 2):
                tok_core(j, delta, True).wait_recv()

    token_plan = {
        3: [(tokens_in, 0)], 5: [(tokens_in, 1)], 6: [(tokens_hop, 0)],
        7: [(tokens_hop, 1)], 8: [(tokens_in, 2), (tokens_last, 0)], 9: [(tokens_last, 1)],
        11: [(tokens_hop, 2)], 12: [(tokens_last, 2)],
    }

    def phase1_start(n):
        for d in (0, 1):
            for item in qz(n, d, 0, 0):
                item.start()
        px_partner(n, mx).start()
        px_mate(n, mx).start()

    def phase1_step(n, s):
        for d in (0, 1):
            for item in qz(n, d, s - 1, 1):
                item.wait_recv()
            for item in qz(n, d, s, 0):
                item.start()
        if s == 1:
            px_partner(n, partner).wait_recv()
            px_forward(n, partner).start()

    def phase2_start(p):
        px_mate(p, mate).wait_recv()
        px_forward(p, across).wait_recv()
        for k in (0, 1):
            for d in (0, 1):
                pzc(p, d, 0, k, 0).start()
        for d in (0, 1):
            for item in qz(p, d, 3, 1):
                item.wait_recv()
        for k in range(4):
            qx_partner(p, k, mx).start()
            qx_mate(p, k, mx).start()

    def phase2_step(p, s):
        for k in (0, 1):
            for d in (0, 1):
                pzc(p, d, s - 1, k, 1).wait_recv()
                if s < 3 or k == d:
                    pzc(p, d, s, k, 0).start()
        for k in ((0,), (1, 2), (3,))[s - 1]:
            qx_partner(p, k, partner).wait_recv()
            qx_forward(p, k, partner).start()

    def phase2_end(p):
        for d in (0, 1):
            pzc(p, d, 3, d, 1).wait_recv()
        for k in range(4):
            qx_mate(p, k, mate).wait_recv()
            qx_forward(p, k, across).wait_recv()

    def project(u, slot, lo, hi):
        if lo == 0:
            acc[...] = jnp.zeros_like(acc)

        def step(pair, carry):
            columns = pl.ds(pl.multiple_of(pair * (DM // 4), 128), DM // 4)
            acc[...] += jnp.dot(
                tokv[slot, :, columns],
                wbuf[u, pl.ds(2 * pair, 2)].reshape(DM // 4, WID),
                preferred_element_type=jnp.float32,
            )
            return carry

        lax.fori_loop(lo, hi, step, 0)

    def activate(u, slot):
        total = acc[...]
        act = (total / (1.0 + jnp.exp(-total))).astype(jnp.bfloat16)
        qkv[u, slot] = act
        if u < 2:
            position = lax.broadcasted_iota(jnp.int32, (TOK, DH), 0) + bases[slot]
            last = start_of(bases[slot] + TOK - 1, ends)
            keys = act[:, :DH]
            kept = jnp.where(position >= last, keys, jnp.zeros_like(keys))
            tails[u, slot] = lax.dot_general(
                kept, act[:, DH:], (((0,), (0,)), ((), ())),
                preferred_element_type=jnp.float32,
            )

    def tail_copy(slot, place):
        source = tails.at[1 - mine, slot]
        return copy(source, t4.at[place], ta, (slot,), to_mate)

    def relay(s):
        return copy(rt.at[s], rt.at[s + 1], rl, (s,), {"z": z_at(1)})

    def inc_copy(slot, receive):
        place = (mate, across)[slot]
        head = 1 - mine if receive else mine
        return copy(inc_send.at[place], inc.at[head, slot], ia, (slot,), to_mate)

    def square_copy(i, side, k):
        return copy(
            sums.at[i, 0], sums.at[i, side * PEERS + k], sq, (i, side, k), peer(side, k)
        )

    def out_copy(i):
        rows = pl.ds(i * TILE, TILE)
        return copy(osend.at[rows, :], orecv.at[rows, :], oe, (i,), to_partner)

    for step in range(16):
        r, s = step // 4, step % 4
        n, p, c = r, r - 1, r - 2
        if s == 0:
            if n < UNITS:
                phase1_start(n)
            if r == 0:
                tok_x(0).start()
                tok_x(1).start()
                for slot in (0, 1):
                    t = lax.broadcasted_iota(jnp.int32, (TOK, 1), 0) + bases[slot]
                    starts[slot] = start_of(t, ends)
            if p >= 0:
                phase2_start(p)
            if r == 1:
                tok_x(2).start()
            if c >= 0:
                phase2_end(c)
        else:
            if n < UNITS:
                phase1_step(n, s)
            if p >= 0:
                phase2_step(p, s)
        for action, j in token_plan.get(step, ()):
            action(j)
        if r == 2:
            if s == 0:
                tok_copy.wait()
            project(0, 0, s, s + 1)
            if s == 3:
                activate(0, 0)
        if step == 12:
            project(1, 0, 0, 4)
            activate(1, 0)
        if step == 13:
            tokens_end()
            project(0, 1, 0, 4)
            activate(0, 1)
        if step == 14:
            project(1, 1, 0, 4)
            activate(1, 1)
        if step == 15:
            tail_copy(0, mx).start()
            tail_copy(1, partner).start()
            for slot, place in ((0, mx), (1, partner)):
                t4[place] = tails[mine, slot]

    def within(j, slot):
        for i in range(TILES):
            rows, width = slice(i * TILE, (i + 1) * TILE), (i + 1) * TILE
            scores = lax.dot_general(
                qkv[2, slot, rows, j * DH:(j + 1) * DH], qkv[j, slot, 0:width, 0:DH],
                (((1,), (1,)), ((), ())), preferred_element_type=jnp.float32,
            )
            t = lax.broadcasted_iota(jnp.int32, (TILE, 1), 0) + (bases[slot] + i * TILE)
            s = lax.broadcasted_iota(jnp.int32, (1, width), 1) + bases[slot]
            keep = (s <= t) & (s >= starts[slot, rows])
            weights = jnp.where(keep, scores, 0.0).astype(jnp.bfloat16)
            mixed[slot, rows, j * DH:(j + 1) * DH] = jnp.dot(
                weights, qkv[j, slot, 0:width, DH:2 * DH], preferred_element_type=jnp.float32
            )

    phase2_end(2)
    tail_copy(0, mate).wait_recv()
    tail_copy(1, across).wait_recv()
    row_last = start_of((mz + 1) * (NX * TOK) - 1, ends)
    total = jnp.zeros((DH, DH), jnp.float32)
    for j in range(NX):
        here = ((mz * NX + j + 1) * TOK - 1 >= row_last).astype(jnp.float32)
        total = total + here * t4[j]
    rt[0] = total
    project(2, 0, 0, 4)
    activate(2, 0)
    relay(0).start()
    project(2, 1, 0, 4)
    activate(2, 1)
    relay(0).wait_recv()
    relay(1).start()
    within(0, 0)
    within(1, 0)
    relay(1).wait_recv()
    relay(2).start()
    within(0, 1)
    relay(2).wait_recv()
    relay(3).start()
    within(1, 1)
    relay(3).wait_recv()

    row_first = start_of(mz * (NX * TOK), ends)
    before = jnp.zeros((DH, DH), jnp.float32)
    for d in range(1, 5):
        row = mz - d
        used = (row >= 0) & ((row + 1) * (NX * TOK) - 1 >= row_first)
        before = before + used.astype(jnp.float32) * rt[d]
    for j in range(NX):
        begin = start_of((mz * NX + j) * TOK, ends)
        state = (begin <= mz * (NX * TOK) - 1).astype(jnp.float32) * before
        for i in range(j):
            used = ((mz * NX + i + 1) * TOK - 1 >= begin).astype(jnp.float32)
            state = state + used * t4[i]
        inc_send[j] = state.astype(jnp.bfloat16)
    for slot in (0, 1):
        inc_copy(slot, False).start()
    for slot, place in ((0, mx), (1, partner)):
        inc[mine, slot] = inc_send[place]
    for slot in (0, 1):
        inc_copy(slot, True).wait_recv()

    def finish_tile(i):
        rows = slice(i * TILE, (i + 1) * TILE)
        for slot in (0, 1):
            carried_on = (starts[slot, rows] <= bases[slot]).astype(jnp.float32)
            squares = jnp.zeros((TILE, DH), jnp.float32)
            for j in (0, 1):
                columns = slice(j * DH, (j + 1) * DH)
                carried = jnp.dot(
                    qkv[2, slot, rows, columns], inc[j, slot],
                    preferred_element_type=jnp.float32,
                )
                value = mixed[slot, rows, columns] + carried * carried_on
                mixed[slot, rows, columns] = value
                squares = squares + value * value
            for a in range(TILE // DH):
                flipped = squares[a * DH:(a + 1) * DH, :].T
                sums[i, 0, slot, a:a + 1, :] = jnp.sum(flipped, axis=0, keepdims=True)
        for side in (0, 1):
            for k in range(PEERS):
                if side or k:
                    square_copy(i, side, k).start()

    gain = gain_ref[:, pl.ds(pl.multiple_of(group * WID, WID), WID)].astype(jnp.float32)
    own_columns = pl.ds(pl.multiple_of(group * WID, WID), WID)
    other_columns = pl.ds(pl.multiple_of((1 - group) * WID, WID), WID)

    def norm_tile(i):
        for side in (0, 1):
            for k in range(PEERS):
                if side or k:
                    square_copy(i, side, k).wait_recv()
        for slot in (1, 0):
            for a in range(TILE // DH):
                total = jnp.zeros((1, DH), jnp.float32)
                for side in (0, 1):
                    for k in range(PEERS):
                        part = sums[i, side * PEERS + k, slot if side == 0 else 1 - slot]
                        total = total + part[a:a + 1, :]
                scale = lax.rsqrt(total / (PEERS * 4 * DH) + 1e-06)
                scale = jnp.broadcast_to(scale, (DH, DH)).T
                rows = slice(i * TILE + a * DH, i * TILE + (a + 1) * DH)
                value = mixed[slot, rows, :]
                value = jnp.concatenate(
                    [value[:, :DH] * scale, value[:, DH:] * scale], axis=1
                )
                value = (value * gain).astype(jnp.bfloat16)
                if slot == 1:
                    osend[rows, :] = value
                else:
                    out_ref[rows, own_columns] = value

    for i in range(TILES):
        finish_tile(i)
    for i in range(TILES):
        norm_tile(i)
        out_copy(i).start()
    for i in range(TILES):
        rows = slice(i * TILE, (i + 1) * TILE)
        out_copy(i).wait_recv()
        out_ref[rows, other_columns] = orecv[rows, :]

    for u in range(UNITS):
        px_mate(u, mx).wait_send()
        px_partner(u, mx).wait_send()
        px_forward(u, partner).wait_send()
        for d in (0, 1):
            for s in range(4):
                for item in qz(u, d, s, 0):
                    item.wait_send()
                for k in (0, 1):
                    if s < 3 or k == d:
                        pzc(u, d, s, k, 0).wait_send()
        for k in range(4):
            qx_mate(u, k, mx).wait_send()
            qx_partner(u, k, mx).wait_send()
            qx_forward(u, k, partner).wait_send()
    for j in range(3):
        tok_x(j).wait_send()
        for d in (0, 1):
            tok_y(j, d, 0, 0).wait_send()
            tok_y(j, d, 1, 0).wait_send()
        for delta in (0, 1, -1, 2):
            tok_core(j, delta, False).wait_send()
    for slot in (0, 1):
        tail_copy(slot, mx).wait_send()
        inc_copy(slot, False).wait_send()
    for s in range(4):
        relay(s).wait_send()
    for i in range(TILES):
        out_copy(i).wait_send()
        for side in (0, 1):
            for k in range(PEERS):
                if side or k:
                    square_copy(i, side, k).wait_send()


def shards(tokens, w_query, w_keyval, doc_lengths, norm_gain):
    halves = []
    for g in (0, 1):
        halves += [w_keyval[:, 2 * g + j, :] for j in (0, 1)]
        halves.append(w_query[:, 2 * g:2 * g + 2, :].reshape(ROWS, WID))
    w_in = jnp.stack(halves).reshape(2, UNITS, ROWS, WID)
    vmem = pl.BlockSpec(memory_space=pltpu.VMEM)
    smem = pl.BlockSpec(memory_space=pltpu.SMEM)
    anywhere = pl.BlockSpec(memory_space=pl.ANY)

    def dma(*shape):
        return pltpu.SemaphoreType.DMA((2, *shape))

    f32, bf16 = jnp.float32, jnp.bfloat16
    return pl.pallas_call(
        kernel,
        out_shape=jax.ShapeDtypeStruct((TOK, 2 * WID), bf16),
        in_specs=[smem, anywhere, anywhere, vmem],
        out_specs=vmem,
        scratch_shapes=[
            pltpu.VMEM((UNITS, NZ, NX, ROWS, WID), bf16),
            pltpu.VMEM((UNITS, NZ, QR, WID), bf16),
            pltpu.VMEM((UNITS, PR, WID), bf16),
            pltpu.VMEM((2, TOK, DM), bf16),
            pltpu.VMEM((TOK, WID), f32),
            pltpu.VMEM((UNITS, 2, TOK, WID), bf16),
            pltpu.VMEM((2, TOK, 1), jnp.int32),
            pltpu.VMEM((2, 2, DH, DH), f32),
            pltpu.VMEM((NX, DH, DH), f32),
            pltpu.VMEM((5, DH, DH), f32),
            pltpu.VMEM((NX, DH, DH), bf16),
            pltpu.VMEM((2, 2, DH, DH), bf16),
            pltpu.VMEM((2, TOK, WID), f32),
            pltpu.VMEM((TILES, 2 * PEERS, 2, 8, DH), f32),
            pltpu.VMEM((TOK, WID), bf16),
            pltpu.VMEM((TOK, WID), bf16),
            pltpu.SemaphoreType.DMA((4,)),
            dma(UNITS), dma(UNITS), dma(UNITS),
            dma(UNITS, 2, 4), dma(UNITS, 2, 4), dma(UNITS, 2, 4, 2),
            dma(UNITS, 4), dma(UNITS, 4), dma(UNITS, 4),
            dma(3), dma(3, 2, 2), dma(3, 4),
            dma(2), dma(4), dma(2), dma(TILES, 2, PEERS), dma(TILES),
        ],
        compiler_params=pltpu.CompilerParams(
            collective_id=0, has_side_effects=True, vmem_limit_bytes=62 << 20
        ),
        name="layer",
    )(doc_lengths, tokens, w_in, norm_gain.reshape(1, 2 * WID))


def solution(mesh):
    grid = Mesh(mesh.devices.reshape(NZ, NX, NY, NC), ("z", "x", "y", "core"))
    seq, fsdp = ("z", "x"), ("y", "core")
    return jax.shard_map(
        shards,
        mesh=grid,
        in_specs=(P(seq, None), P(seq, fsdp, None), P(seq, fsdp, None), P(), P(fsdp)),
        out_specs=P(seq, fsdp),
        check_vma=False,
    )
```

time: 429 us -> 141 us (0.33)
  waiting for transfers between devices: 201 us -> 0 us
  Pallas kernels: 0 us -> 133 us
  blocking collectives: 71.8 us -> 0 us
  other arithmetic: 39.8 us -> 0 us
  local copies, waits for them, and re-layouts: 41.2 us -> 7.07 us
  matrix products: 33.1 us -> 0 us
  loops' own time: 22.3 us -> 0 us
  between operations: 17.7 us -> 0.08 us
    all_gather x3 -> x0, waiting for transfers between devices: 200 us -> none  [the longest x1 121 us: shards(): keyval_sum = project(lax.all_gather(w_keyval, 'seq', axis=0, tiled=True))]
    pallas_call x0 -> x1, Pallas kernels: none -> 133 us  [shards(): pl.pallas_call(kernel, out_shape=jax.ShapeDtypeStruct((TOK, 2 * WID), bf1...]
    unnamed x1 -> x0, blocking collectives: 58.6 us -> none
    select_n x31 -> x0, other arithmetic: 35.6 us -> none  [step(): jnp.where(position < mine, new, old)]
    dot_general x5 -> x0, matrix products: 33.1 us -> none  [the longest x2 23.1 us: project(): return jnp.dot(tokens, panel, preferred_element_type=jnp.float32)]
    another operation x1 -> x0, loops' own time: 22.3 us -> none  [carried_in(): return lax.fori_loop(0, count - 1, step, running)]
    dynamic_slice x33 -> x0, local copies, waits for them, and re-layouts: 21.8 us -> none  [the longest x31 20.6 us: step(): longer = join(running, jax.tree.map(lambda part: part[position], pieces))]
    psum x1 -> x0, blocking collectives: 13.2 us -> none  [shards(): sum_squares = lax.psum(jnp.sum(mixed * mixed, axis=(1, 2)), 'fsdp')]
  transfers between devices with their start and end apart: 3 -> 0, of which waited for: 2 -> 0; matrix products, arithmetic and copies ran while one was open for 11% -> 0% of each run, Pallas kernels for 0% -> 0%
where the time goes in v2:
time: 141 us; the launch traced here: 140 us
  Pallas kernels  133 us (94%)
  local copies, waits for them, and re-layouts  7.07 us (5%)
    pallas_call x1, Pallas kernels, shards(): pl.pallas_call(kernel, out_shape=jax.ShapeDtypeStruct((TOK, 2 * WID), bf1...  133 us

profile of v2, /device:TPU:1, one launch (start us, length us, event | category | flops | bytes accessed | tf_op | source)
XLA Modules:
  0.0 140.5 jit_solution(1138625535299048150)
XLA Ops:
  0.0 2.3 %fusion.4 = (bf16[192,1,256]{2,1,0:T(2,128)(2,1)S(1)}, bf16[192,1,256]{2,1,0:T(2,128)(2,1)S(1)}, bf16[192,1,256]{2,1,0:T(2,128)(2,1)S(1)}, bf16[192,1,256]{2,1,0:T(2,128)(2,1)S(1)}) fusion(bf16[192,4,256]{2,1,0:T(4,128)(2,1)} %param.7), kind=kLoop, calls=%fused_computation.10 | loop fusion | bytes 786432 | tf_op jit(solution)/shard_map/slice | solution.py:506
  2.4 1.2 fusion.5
  3.6 0.1 stack_reshape.6
  3.7 0.1 stack_reshape.7
  3.8 0.0 copy-start
  3.8 1.3 reshape.7.gain_ref
  5.1 0.0 copy-done
  5.1 133.3 %layer.1 = bf16[768,512]{1,0:T(8,128)(2,1)} custom-call(s32[8]{0:T(128)} %len_ref.1, bf16[768,6144]{1,0:T(8,128)(2,1)} %tok_hbm.1, bf16[2,3,192,256]{3,2,1,0:T(8,128)(2,1)} %bitcast.17, bf16[1,512]{1,0:T(2,128)(2,1)} %reshape.7.gain_ref), custom_call_target="tpu_custom_call" | custom-call | tf_op jit(solution)/shard_map/layer/pallas_call | solution.py:517
  138.4 2.1 %copy.35 = bf16[768,512]{1,0:T(8,128)(2,1)} copy(bf16[768,512]{1,0:T(8,128)(2,1)} %layer.1) | data formatting | bytes 1572864
  (6 shorter events, 0.1 us)
Async XLA Ops:
  3.8 1.3 copy-start

commit v3 on v2

v3 whole, which is shorter than its diff:
```python
import jax
import jax.numpy as jnp
from jax import lax
from jax.experimental import pallas as pl
from jax.experimental.pallas import tpu as pltpu
from jax.sharding import Mesh, PartitionSpec as P

NZ, NX, NY, NC = 8, 4, 4, 2
PEERS = NY * NC
UNITS = 3
ROWS = 192
PR = 80
QR = ROWS - PR
WID = 256
TOK = 768
DM = 6144
DH = 128
PIECE = TOK // PEERS
SUBS = 6
SUB = PIECE // SUBS
STEPS = 16
TILE = 256
TILES = TOK // TILE
MESH = pl.DeviceIdType.MESH


def doc_ends(len_ref):
    ends, total = [], jnp.int32(0)
    for i in range(8):
        total = total + len_ref[i]
        ends.append(total)
    return ends


def start_of(position, ends):
    start = jnp.zeros_like(position)
    for end in ends:
        start = jnp.maximum(start, jnp.where(position >= end, end, 0))
    return start


def kernel(
    len_ref, tok_hbm, w_hbm, gain_ref, out_ref,
    wbuf, tbuf, tpb, tokv, acc, qkv, starts, tails, t4, rt, inc_send, inc,
    mixed, sums, sends, osend, orecv, local_sem,
    pxm, pxp, pxf, qzm, qzt, pz, qxm, qxp, qxf, t1, t2, t3,
    ta, rl, ia, sq, oe,
):
    mz, mx = lax.axis_index("z"), lax.axis_index("x")
    my, mc = lax.axis_index("y"), lax.axis_index("core")
    me = my * NC + mc
    mate = mx + 1 - 2 * lax.rem(mx, 2)
    partner = NX - 1 - mx
    across = NX - 1 - mate
    group = mx // 2
    mine = lax.rem(mx, 2)
    ends = doc_ends(len_ref)
    blocks = (mz * NX + mx, mz * NX + partner)
    bases = (blocks[0] * TOK, blocks[1] * TOK)

    stage = (
        pltpu.make_async_copy(w_hbm.at[group], wbuf.at[:, mz, mx], local_sem.at[0]),
        pltpu.make_async_copy(
            w_hbm.at[1 - group, :, pl.ds(PR, QR), :], tbuf.at[:, mz], local_sem.at[1]
        ),
        pltpu.make_async_copy(w_hbm.at[1 - group, :, pl.ds(0, PR), :], tpb, local_sem.at[2]),
    )
    for item in stage:
        item.start()
    tok_copy = pltpu.make_async_copy(tok_hbm, tokv.at[0], local_sem.at[3])
    tok_copy.start()

    def z_at(delta):
        return lax.rem(mz + delta + NZ, NZ)

    def y_at(delta):
        return lax.rem(my + delta + NY, NY)

    def peer(side, k):
        index = lax.rem(me + k, PEERS)
        return {
            "x": mx if side == 0 else partner,
            "y": index // NC,
            "core": lax.rem(index, NC),
        }

    barrier = pltpu.get_barrier_semaphore()

    def greet(target):
        pl.semaphore_signal(barrier, inc=1, device_id=target, device_id_type=MESH)

    greet({"x": mate})
    for delta in (1, -1, 3, -3):
        greet({"z": z_at(delta)})
    for k in range(PEERS):
        if k:
            greet(peer(0, k))
        greet(peer(1, k))
    pl.semaphore_wait(barrier, 5 + 2 * PEERS - 1)
    for item in stage:
        item.wait()

    def copy(src, dst, sems, index, target):
        return pltpu.make_async_remote_copy(
            src_ref=src, dst_ref=dst, send_sem=sems.at[(0, *index)],
            recv_sem=sems.at[(1, *index)], device_id=target, device_id_type=MESH,
        )

    def same(ref, sems, index, target):
        return copy(ref, ref, sems, index, target)

    to_mate, to_partner = {"x": mate}, {"x": partner}

    def upper(u, x):
        return wbuf.at[u, mz, x, pl.ds(0, PR), :]

    def px_mate(u, x):
        return same(upper(u, x), pxm, (u,), to_mate)

    def px_partner(u, x):
        return copy(tpb.at[u], upper(u, x), pxp, (u,), to_partner)

    def px_forward(u, x):
        return same(upper(u, x), pxf, (u,), to_mate)

    def qz(u, d, s, lag):
        sign = 1 - 2 * d
        block = z_at(-sign * (s + lag))
        lo, size = (0, QR) if s < 3 else ((0, 48) if d == 0 else (48, QR - 48))
        target = {"z": z_at(sign)}
        return (
            same(wbuf.at[u, block, mx, pl.ds(PR + lo, size), :], qzm, (u, d, s), target),
            same(tbuf.at[u, block, pl.ds(lo, size), :], qzt, (u, d, s), target),
        )

    def pzc(u, d, s, k, lag):
        sign = 1 - 2 * d
        block = z_at(-sign * (s + lag))
        pair = group if k == 0 else 1 - group
        return same(
            wbuf.at[u, block, pl.ds(2 * pair, 2), pl.ds(0, PR), :],
            pz, (u, d, s, k), {"z": z_at(sign)},
        )

    def block_at(i):
        if i == 0:
            return mz
        distance = (i + 1) // 2
        return z_at(-distance if i % 2 else distance)

    def lower(u, i, x):
        return wbuf.at[u, block_at(i), x, pl.ds(PR, QR), :]

    def qx_mate(u, i, x):
        return same(lower(u, i, x), qxm, (u, i), to_mate)

    def qx_partner(u, i, x):
        return copy(tbuf.at[u, block_at(i)], lower(u, i, x), qxp, (u, i), to_partner)

    def qx_forward(u, i, x):
        return same(lower(u, i, x), qxf, (u, i), to_mate)

    def token_rows(y, core, j):
        return tokv.at[1, pl.ds((y * NC + core) * PIECE + j * SUB, SUB), :]

    def tok_x(j):
        start = me * PIECE + j * SUB
        return copy(tok_hbm.at[pl.ds(start, SUB), :], token_rows(my, mc, j), t1, (j,), to_partner)

    def tok_y(j, d, s, lag):
        sign = 1 - 2 * d
        return same(
            token_rows(y_at(-sign * (s + lag)), mc, j), t2, (j, d, s), {"y": y_at(sign)}
        )

    def tok_core(j, delta, receive):
        core = 1 - mc if receive else mc
        return same(token_rows(y_at(delta), core, j), t3, (j, delta % NY), {"core": 1 - mc})

    def tokens_in(j):
        tok_x(j).wait_recv()
        for d in (0, 1):
            tok_y(j, d, 0, 0).start()
        tok_core(j, 0, False).start()

    def tokens_hop(j):
        for d in (0, 1):
            tok_y(j, d, 0, 1).wait_recv()
        tok_y(j, j % 2, 1, 0).start()
        for delta in (1, -1):
            tok_core(j, delta, False).start()

    def tokens_last(j):
        tok_y(j, j % 2, 1, 1).wait_recv()
        tok_core(j, 2, False).start()

    def tokens_end():
        for j in range(SUBS):
            for delta in (0, 1, -1, 2):
                tok_core(j, delta, True).wait_recv()

    token_plan = {
        2: [(tokens_in, 0)], 3: [(tokens_in, 1), (tokens_in, 2)],
        4: [(tokens_in, 3), (tokens_hop, 0)], 5: [(tokens_in, 4), (tokens_hop, 1)],
        6: [(tokens_in, 5), (tokens_last, 0), (tokens_hop, 2)],
        7: [(tokens_last, 1), (tokens_hop, 3)], 8: [(tokens_last, 2), (tokens_hop, 4)],
        9: [(tokens_last, 3), (tokens_hop, 5)], 10: [(tokens_last, 4), (tokens_last, 5)],
    }
    token_sends = {0: (0, 1), 1: (2,), 2: (3,), 3: (4,), 4: (5,)}

    def arrivals(step):
        return {0: (0,), 1: (1, 2), 2: (3, 4), 3: (5, 6), 4: (7,)}.get(step, ())

    def events(u, s):
        lag = 1 if u < 2 else 0
        if s == 0:
            px_partner(u, mx).start()
            px_mate(u, mx).start()
        if 1 <= s <= 4:
            for d in (0, 1):
                for item in qz(u, d, s - 1, 1):
                    item.wait_recv()
        if s <= 3:
            for d in (0, 1):
                for item in qz(u, d, s, 0):
                    item.start()
        for i in arrivals(s):
            qx_partner(u, i, mx).start()
            qx_mate(u, i, mx).start()
        if s == 1:
            px_partner(u, partner).wait_recv()
            px_forward(u, partner).start()
        for k in (0, 1):
            hop = s - 1 - k
            if hop == 0:
                if k == 0:
                    px_mate(u, mate).wait_recv()
                else:
                    px_forward(u, across).wait_recv()
            for d in (0, 1):
                if 1 <= hop <= 3 or (hop == 4 and k == d):
                    pzc(u, d, hop - 1, k, 1).wait_recv()
                if 0 <= hop <= 2 or (hop == 3 and k == d):
                    pzc(u, d, hop, k, 0).start()
        for i in arrivals(s - 2 - lag):
            qx_partner(u, i, partner).wait_recv()
            qx_forward(u, i, partner).start()

    def arrived(u, group_at):
        for i in arrivals(group_at):
            qx_mate(u, i, mate).wait_recv()
            qx_forward(u, i, across).wait_recv()

    def product(u, slot, block):
        columns = pl.ds(pl.multiple_of(block * (DM // NZ), DH), DM // NZ)
        return jnp.dot(
            tokv[slot, :, columns], wbuf[u, block].reshape(DM // NZ, WID),
            preferred_element_type=jnp.float32,
        )

    def project(u, slots, group_at):
        if group_at == 0:
            for slot in slots:
                acc[slot] = product(u, slot, mz)
            return
        sides = len(arrivals(group_at))

        def step(index, carry):
            slot = index // sides if len(slots) == 2 else slots[0]
            sign = 1 - 2 * lax.rem(index, sides)
            acc[slot] += product(u, slot, lax.rem(mz + sign * group_at + NZ, NZ))
            return carry

        lax.fori_loop(0, sides * len(slots), step, 0)

    def project_all(u, slot):
        acc[slot] = product(u, slot, 0)

        def step(block, carry):
            acc[slot] += product(u, slot, block)
            return carry

        lax.fori_loop(1, NZ, step, 0)

    def activate(u, slot):
        total = acc[slot]
        act = (total / (1.0 + jnp.exp(-total))).astype(jnp.bfloat16)
        qkv[u, slot] = act
        if u < 2:
            position = lax.broadcasted_iota(jnp.int32, (TOK, DH), 0) + bases[slot]
            last = start_of(bases[slot] + TOK - 1, ends)
            keys = act[:, :DH]
            kept = jnp.where(position >= last, keys, jnp.zeros_like(keys))
            tails[u, slot] = lax.dot_general(
                kept, act[:, DH:], (((0,), (0,)), ((), ())),
                preferred_element_type=jnp.float32,
            )

    def tail_copy(slot, place):
        source = tails.at[1 - mine, slot]
        return copy(source, t4.at[place], ta, (slot,), to_mate)

    def relay(s):
        if s == 0:
            return copy(rt.at[0], rt.at[1], rl, (0,), {"z": z_at(1)})
        return copy(rt.at[2], rt.at[2 + s], rl, (s,), {"z": z_at(1 if s == 1 else 3)})

    def inc_copy(slot, receive):
        place = (mate, across)[slot]
        head = 1 - mine if receive else mine
        return copy(inc_send.at[place], inc.at[head, slot], ia, (slot,), to_mate)

    def square_copy(side, k):
        return copy(
            sends.at[side], sums.at[side * PEERS + k], sq, (side, k), peer(side, k)
        )

    def out_copy(i):
        rows = pl.ds(i * TILE, TILE)
        return copy(osend.at[rows, :], orecv.at[rows, :], oe, (i,), to_partner)

    def row_tail():
        tail_copy(0, mate).wait_recv()
        tail_copy(1, across).wait_recv()
        row_last = start_of((mz + 1) * (NX * TOK) - 1, ends)
        total = jnp.zeros((DH, DH), jnp.float32)
        for j in range(NX):
            here = ((mz * NX + j + 1) * TOK - 1 >= row_last).astype(jnp.float32)
            total = total + here * t4[j]
        rt[0] = total

    def row_pair():
        relay(0).wait_recv()
        row_last = start_of((mz + 1) * (NX * TOK) - 1, ends)
        kept = (mz >= 1) & (mz * (NX * TOK) - 1 >= row_last)
        rt[2] = rt[0] + kept.astype(jnp.float32) * rt[1]

    for step in range(STEPS):
        for u in reversed(range(UNITS)):
            if 0 <= step - 4 * u <= 7:
                events(u, step - 4 * u)
        for j in token_sends.get(step, ()):
            tok_x(j).start()
        for action, j in token_plan.get(step, ()):
            action(j)
        if step == 13:
            tail_copy(0, mx).start()
            tail_copy(1, partner).start()
        if step == 14:
            relay(0).start()
        if step == 15:
            relay(1).start()
            relay(2).start()
        if step == 0:
            for slot in (0, 1):
                t = lax.broadcasted_iota(jnp.int32, (TOK, 1), 0) + bases[slot]
                starts[slot] = start_of(t, ends)
        if step == 4:
            tok_copy.wait()
        for u in (0, 1):
            part = step - 4 * u - 4
            if 0 <= part <= 4:
                arrived(u, part)
                project(u, (0,), part)
                if part == 4:
                    activate(u, 0)
        if step == 11:
            tokens_end()
            project_all(0, 1)
            activate(0, 1)
        if step == 12:
            project_all(1, 1)
            activate(1, 1)
            parts = (0, 1)
        else:
            parts = (step - 11,) if step > 12 else ()
        for part in parts:
            arrived(2, part)
            project(2, (1, 0), part)
        if step == 13:
            for slot, place in ((0, mx), (1, partner)):
                t4[place] = tails[mine, slot]
            row_tail()
        if step == 14:
            row_pair()
    activate(2, 1)
    activate(2, 0)

    def within(j, slot):
        for i in range(TILES):
            rows, width = slice(i * TILE, (i + 1) * TILE), (i + 1) * TILE
            scores = lax.dot_general(
                qkv[2, slot, rows, j * DH:(j + 1) * DH], qkv[j, slot, 0:width, 0:DH],
                (((1,), (1,)), ((), ())), preferred_element_type=jnp.float32,
            )
            t = lax.broadcasted_iota(jnp.int32, (TILE, 1), 0) + (bases[slot] + i * TILE)
            s = lax.broadcasted_iota(jnp.int32, (1, width), 1) + bases[slot]
            keep = (s <= t) & (s >= starts[slot, rows])
            weights = jnp.where(keep, scores, 0.0).astype(jnp.bfloat16)
            mixed[slot, rows, j * DH:(j + 1) * DH] = jnp.dot(
                weights, qkv[j, slot, 0:width, DH:2 * DH], preferred_element_type=jnp.float32
            )

    for slot in (1, 0):
        within(0, slot)
        within(1, slot)
    relay(1).wait_recv()
    relay(2).wait_recv()
    row_first = start_of(mz * (NX * TOK), ends)
    before = jnp.zeros((DH, DH), jnp.float32)
    for d, at in ((1, 3), (3, 4)):
        row = mz - d
        used = (row >= 0) & ((row + 1) * (NX * TOK) - 1 >= row_first)
        before = before + used.astype(jnp.float32) * rt[at]
    for j in range(NX):
        begin = start_of((mz * NX + j) * TOK, ends)
        state = (begin <= mz * (NX * TOK) - 1).astype(jnp.float32) * before
        for i in range(j):
            used = ((mz * NX + i + 1) * TOK - 1 >= begin).astype(jnp.float32)
            state = state + used * t4[i]
        inc_send[j] = state.astype(jnp.bfloat16)
    for slot in (0, 1):
        inc_copy(slot, False).start()
    for slot, place in ((0, mx), (1, partner)):
        inc[mine, slot] = inc_send[place]
    for slot in (0, 1):
        inc_copy(slot, True).wait_recv()

    def finish_tile(slot, i):
        rows = slice(i * TILE, (i + 1) * TILE)
        carried_on = (starts[slot, rows] <= bases[slot]).astype(jnp.float32)
        squares = jnp.zeros((TILE, DH), jnp.float32)
        for j in (0, 1):
            columns = slice(j * DH, (j + 1) * DH)
            carried = jnp.dot(
                qkv[2, slot, rows, columns], inc[j, slot], preferred_element_type=jnp.float32
            )
            value = mixed[slot, rows, columns] + carried * carried_on
            if slot == 0:
                mixed[slot, rows, columns] = value
            else:
                osend[rows, columns] = value.astype(jnp.bfloat16)
            squares = squares + value * value
        for a in range(TILE // DH):
            flipped = squares[a * DH:(a + 1) * DH, :].T
            row = i * (TILE // DH) + a
            sends[slot, row:row + 1, :] = jnp.sum(flipped, axis=0, keepdims=True)

    for slot in (0, 1):
        sends[slot, TOK // DH:8, :] = jnp.zeros((8 - TOK // DH, DH), jnp.float32)
    for i in range(TILES):
        finish_tile(1, i)
        if i:
            out_copy(i - 1).start()
    for k in range(PEERS):
        square_copy(1, k).start()
    out_copy(TILES - 1).start()
    for i in range(TILES):
        finish_tile(0, i)
    for k in range(1, PEERS):
        square_copy(0, k).start()
    gain = gain_ref[...].astype(jnp.float32)
    own_columns = pl.ds(pl.multiple_of(group * WID, WID), WID)
    other_columns = pl.ds(pl.multiple_of((1 - group) * WID, WID), WID)
    is_first = (group == 0).astype(jnp.float32)
    own_gain = gain[:, :WID] * is_first + gain[:, WID:] * (1.0 - is_first)
    other_gain = gain[:, WID:] * is_first + gain[:, :WID] * (1.0 - is_first)
    for side in (0, 1):
        for k in range(PEERS):
            if side or k:
                square_copy(side, k).wait_recv()
    total = sends[0]
    for index in range(1, 2 * PEERS):
        total = total + sums[index]
    inverse = lax.rsqrt(total / (PEERS * 4 * DH) + 1e-06)
    scales = [
        jnp.broadcast_to(inverse[a:a + 1, :], (DH, DH)).T for a in range(TOK // DH)
    ]

    def write(columns, source, factor, a):
        rows = slice(a * DH, (a + 1) * DH)
        value = source[rows, :].astype(jnp.float32)
        value = jnp.concatenate(
            [value[:, :DH] * scales[a], value[:, DH:] * scales[a]], axis=1
        )
        out_ref[rows, columns] = (value * factor).astype(jnp.bfloat16)

    for a in range(TOK // DH):
        write(own_columns, mixed.at[0], own_gain, a)
    for i in range(TILES):
        out_copy(i).wait_recv()
        for a in (2 * i, 2 * i + 1):
            write(other_columns, orecv, other_gain, a)

    for u in range(UNITS):
        px_mate(u, mx).wait_send()
        px_partner(u, mx).wait_send()
        px_forward(u, partner).wait_send()
        for d in (0, 1):
            for s in range(4):
                for item in qz(u, d, s, 0):
                    item.wait_send()
                for k in (0, 1):
                    if s < 3 or k == d:
                        pzc(u, d, s, k, 0).wait_send()
        for i in range(NZ):
            qx_mate(u, i, mx).wait_send()
            qx_partner(u, i, mx).wait_send()
            qx_forward(u, i, partner).wait_send()
    for j in range(SUBS):
        tok_x(j).wait_send()
        for d in (0, 1):
            tok_y(j, d, 0, 0).wait_send()
        tok_y(j, j % 2, 1, 0).wait_send()
        for delta in (0, 1, -1, 2):
            tok_core(j, delta, False).wait_send()
    for slot in (0, 1):
        tail_copy(slot, mx).wait_send()
        inc_copy(slot, False).wait_send()
    for s in range(3):
        relay(s).wait_send()
    for i in range(TILES):
        out_copy(i).wait_send()
    for side in (0, 1):
        for k in range(PEERS):
            if side or k:
                square_copy(side, k).wait_send()


def shards(tokens, w_query, w_keyval, doc_lengths, norm_gain):
    halves = []
    for g in (0, 1):
        halves += [w_keyval[:, 2 * g + j, :] for j in (0, 1)]
        halves.append(w_query[:, 2 * g:2 * g + 2, :].reshape(ROWS, WID))
    w_in = jnp.stack(halves).reshape(2, UNITS, ROWS, WID)
    vmem = pl.BlockSpec(memory_space=pltpu.VMEM)
    smem = pl.BlockSpec(memory_space=pltpu.SMEM)
    anywhere = pl.BlockSpec(memory_space=pl.ANY)

    def dma(*shape):
        return pltpu.SemaphoreType.DMA((2, *shape))

    f32, bf16 = jnp.float32, jnp.bfloat16
    return pl.pallas_call(
        kernel,
        out_shape=jax.ShapeDtypeStruct((TOK, 2 * WID), bf16),
        in_specs=[smem, anywhere, anywhere, vmem],
        out_specs=vmem,
        scratch_shapes=[
            pltpu.VMEM((UNITS, NZ, NX, ROWS, WID), bf16),
            pltpu.VMEM((UNITS, NZ, QR, WID), bf16),
            pltpu.VMEM((UNITS, PR, WID), bf16),
            pltpu.VMEM((2, TOK, DM), bf16),
            pltpu.VMEM((2, TOK, WID), f32),
            pltpu.VMEM((UNITS, 2, TOK, WID), bf16),
            pltpu.VMEM((2, TOK, 1), jnp.int32),
            pltpu.VMEM((2, 2, DH, DH), f32),
            pltpu.VMEM((NX, DH, DH), f32),
            pltpu.VMEM((5, DH, DH), f32),
            pltpu.VMEM((NX, DH, DH), bf16),
            pltpu.VMEM((2, 2, DH, DH), bf16),
            pltpu.VMEM((2, TOK, WID), f32),
            pltpu.VMEM((2 * PEERS, 8, DH), f32),
            pltpu.VMEM((2, 8, DH), f32),
            pltpu.VMEM((TOK, WID), bf16),
            pltpu.VMEM((TOK, WID), bf16),
            pltpu.SemaphoreType.DMA((4,)),
            dma(UNITS), dma(UNITS), dma(UNITS),
            dma(UNITS, 2, 4), dma(UNITS, 2, 4), dma(UNITS, 2, 4, 2),
            dma(UNITS, NZ), dma(UNITS, NZ), dma(UNITS, NZ),
            dma(SUBS), dma(SUBS, 2, 2), dma(SUBS, NY),
            dma(2), dma(3), dma(2), dma(2, PEERS), dma(TILES),
        ],
        compiler_params=pltpu.CompilerParams(
            collective_id=0, has_side_effects=True, vmem_limit_bytes=62 << 20
        ),
        name="layer",
    )(doc_lengths, tokens, w_in, norm_gain.reshape(1, 2 * WID))


def solution(mesh):
    grid = Mesh(mesh.devices.reshape(NZ, NX, NY, NC), ("z", "x", "y", "core"))
    seq, fsdp = ("z", "x"), ("y", "core")
    return jax.shard_map(
        shards,
        mesh=grid,
        in_specs=(P(seq, None), P(seq, fsdp, None), P(seq, fsdp, None), P(), P(fsdp)),
        out_specs=P(seq, fsdp),
        check_vma=False,
    )
```

time: 141 us -> 132 us (0.936)
  Pallas kernels: 133 us -> 125 us
    pallas_call x1, Pallas kernels: 133 us -> 125 us  [shards(): pl.pallas_call(kernel, out_shape=jax.ShapeDtypeStruct((TOK, 2 * WID), bf1...]
where the time goes in v3:
time: 132 us
  Pallas kernels  125 us (95%)
  local copies, waits for them, and re-layouts  7.07 us (5%)
    pallas_call x1, Pallas kernels, shards(): pl.pallas_call(kernel, out_shape=jax.ShapeDtypeStruct((TOK, 2 * WID), bf1...  125 us

profile of v3, /device:TPU:1, one launch (start us, length us, event | category | flops | bytes accessed | tf_op | source)
XLA Modules:
  0.0 132.2 jit_solution(17726781642838753001)
XLA Ops:
  0.0 2.3 %fusion.4 = (bf16[192,1,256]{2,1,0:T(2,128)(2,1)S(1)}, bf16[192,1,256]{2,1,0:T(2,128)(2,1)S(1)}, bf16[192,1,256]{2,1,0:T(2,128)(2,1)S(1)}, bf16[192,1,256]{2,1,0:T(2,128)(2,1)S(1)}) fusion(bf16[192,4,256]{2,1,0:T(4,128)(2,1)} %param.7), kind=kLoop, calls=%fused_computation.10 | loop fusion | bytes 786432 | tf_op jit(solution)/shard_map/slice | solution.py:533
  2.4 1.2 fusion.5
  3.6 0.1 stack_reshape.6
  3.7 0.1 stack_reshape.7
  3.8 0.0 copy-start
  3.8 1.3 reshape.7.gain_ref
  5.1 0.0 copy-done
  5.1 125.1 %layer.1 = bf16[768,512]{1,0:T(8,128)(2,1)} custom-call(s32[8]{0:T(128)} %len_ref.1, bf16[768,6144]{1,0:T(8,128)(2,1)} %tok_hbm.1, bf16[2,3,192,256]{3,2,1,0:T(8,128)(2,1)} %bitcast.17, bf16[1,512]{1,0:T(2,128)(2,1)} %reshape.7.gain_ref), custom_call_target="tpu_custom_call" | custom-call | tf_op jit(solution)/shard_map/layer/pallas_call | solution.py:544
  130.2 2.1 %copy.35 = bf16[768,512]{1,0:T(8,128)(2,1)} copy(bf16[768,512]{1,0:T(8,128)(2,1)} %layer.1) | data formatting | bytes 1572864
  (6 shorter events, 0.1 us)
Async XLA Ops:
  3.8 1.3 copy-start

commit v4 on v3

--- a/solution.py
+++ b/solution.py
@@ -40,7 +40,7 @@
 
 
 def kernel(
-    len_ref, tok_hbm, w_hbm, gain_ref, out_ref,
+    len_ref, tok_hbm, wkv_hbm, wq_hbm, gain_ref, out_ref,
     wbuf, tbuf, tpb, tokv, acc, qkv, starts, tails, t4, rt, inc_send, inc,
     mixed, sums, sends, osend, orecv, local_sem,
     pxm, pxp, pxf, qzm, qzt, pz, qxm, qxp, qxf, t1, t2, t3,
@@ -58,13 +58,24 @@
     blocks = (mz * NX + mx, mz * NX + partner)
     bases = (blocks[0] * TOK, blocks[1] * TOK)
 
-    stage = (
-        pltpu.make_async_copy(w_hbm.at[group], wbuf.at[:, mz, mx], local_sem.at[0]),
-        pltpu.make_async_copy(
-            w_hbm.at[1 - group, :, pl.ds(PR, QR), :], tbuf.at[:, mz], local_sem.at[1]
-        ),
-        pltpu.make_async_copy(w_hbm.at[1 - group, :, pl.ds(0, PR), :], tpb, local_sem.at[2]),
-    )
+    def staged(index, source, target):
+        return pltpu.make_async_copy(source, target, local_sem.at[index])
+
+    kv_mine = wkv_hbm.at[pl.ds(2 * group, 2)]
+    kv_other = wkv_hbm.at[pl.ds(2 * (1 - group), 2)]
+    stage = [
+        staged(0, kv_mine, wbuf.at[pl.ds(0, 2), mz, mx]),
+        staged(1, kv_other.at[:, pl.ds(PR, QR), :], tbuf.at[pl.ds(0, 2), mz]),
+        staged(2, kv_other.at[:, pl.ds(0, PR), :], tpb.at[pl.ds(0, 2)]),
+    ]
+    for j in (0, 1):
+        columns = pl.ds(j * DH, DH)
+        q_mine, q_other = wq_hbm.at[2 * group + j], wq_hbm.at[2 * (1 - group) + j]
+        stage += [
+            staged(4 + 3 * j, q_mine, wbuf.at[2, mz, mx, :, columns]),
+            staged(5 + 3 * j, q_other.at[pl.ds(PR, QR), :], tbuf.at[2, mz, :, columns]),
+            staged(6 + 3 * j, q_other.at[pl.ds(0, PR), :], tpb.at[2, :, columns]),
+        ]
     for item in stage:
         item.start()
     tok_copy = pltpu.make_async_copy(tok_hbm, tokv.at[0], local_sem.at[3])
@@ -109,37 +120,54 @@
     def same(ref, sems, index, target):
         return copy(ref, ref, sems, index, target)
 
+    def unit_copy(src, dst, sems, u, rest, target):
+        return pltpu.make_async_remote_copy(
+            src_ref=src, dst_ref=dst, send_sem=sems.at[(0, *rest)],
+            recv_sem=sems.at[(1 + u, *rest)], device_id=target, device_id_type=MESH,
+        )
+
+    def unit_same(ref, sems, u, rest, target):
+        return unit_copy(ref, ref, sems, u, rest, target)
+
+    def send(make, u, *args):
+        if u:
+            make(u - 1, *args).wait_send()
+        make(u, *args).start()
+
     to_mate, to_partner = {"x": mate}, {"x": partner}
 
     def upper(u, x):
         return wbuf.at[u, mz, x, pl.ds(0, PR), :]
 
     def px_mate(u, x):
-        return same(upper(u, x), pxm, (u,), to_mate)
+        return unit_same(upper(u, x), pxm, u, (), to_mate)
 
     def px_partner(u, x):
-        return copy(tpb.at[u], upper(u, x), pxp, (u,), to_partner)
+        return unit_copy(tpb.at[u], upper(u, x), pxp, u, (), to_partner)
 
     def px_forward(u, x):
-        return same(upper(u, x), pxf, (u,), to_mate)
-
-    def qz(u, d, s, lag):
+        return unit_same(upper(u, x), pxf, u, (), to_mate)
+
+    def qz_part(d, s, lag):
         sign = 1 - 2 * d
-        block = z_at(-sign * (s + lag))
         lo, size = (0, QR) if s < 3 else ((0, 48) if d == 0 else (48, QR - 48))
-        target = {"z": z_at(sign)}
-        return (
-            same(wbuf.at[u, block, mx, pl.ds(PR + lo, size), :], qzm, (u, d, s), target),
-            same(tbuf.at[u, block, pl.ds(lo, size), :], qzt, (u, d, s), target),
-        )
+        return z_at(-sign * (s + lag)), lo, size, {"z": z_at(sign)}
+
+    def qz_mine(u, d, s, lag):
+        block, lo, size, target = qz_part(d, s, lag)
+        return unit_same(wbuf.at[u, block, mx, pl.ds(PR + lo, size), :], qzm, u, (d, s), target)
+
+    def qz_other(u, d, s, lag):
+        block, lo, size, target = qz_part(d, s, lag)
+        return unit_same(tbuf.at[u, block, pl.ds(lo, size), :], qzt, u, (d, s), target)
 
     def pzc(u, d, s, k, lag):
         sign = 1 - 2 * d
         block = z_at(-sign * (s + lag))
         pair = group if k == 0 else 1 - group
-        return same(
+        return unit_same(
             wbuf.at[u, block, pl.ds(2 * pair, 2), pl.ds(0, PR), :],
-            pz, (u, d, s, k), {"z": z_at(sign)},
+            pz, u, (d, s, k), {"z": z_at(sign)},
         )
 
     def block_at(i):
@@ -152,13 +180,15 @@
         return wbuf.at[u, block_at(i), x, pl.ds(PR, QR), :]
 
     def qx_mate(u, i, x):
-        return same(lower(u, i, x), qxm, (u, i), to_mate)
+        return unit_same(lower(u, i, x), qxm, u, (i,), to_mate)
 
     def qx_partner(u, i, x):
-        return copy(tbuf.at[u, block_at(i)], lower(u, i, x), qxp, (u, i), to_partner)
+        return unit_copy(
+            tbuf.at[u, block_at(i)], lower(u, i, x), qxp, u, (i,), to_partner
+        )
 
     def qx_forward(u, i, x):
-        return same(lower(u, i, x), qxf, (u, i), to_mate)
+        return unit_same(lower(u, i, x), qxf, u, (i,), to_mate)
 
     def token_rows(y, core, j):
         return tokv.at[1, pl.ds((y * NC + core) * PIECE + j * SUB, SUB), :]
@@ -170,7 +200,8 @@
     def tok_y(j, d, s, lag):
         sign = 1 - 2 * d
         return same(
-            token_rows(y_at(-sign * (s + lag)), mc, j), t2, (j, d, s), {"y": y_at(sign)}
+            token_rows(y_at(-sign * (s + lag)), mc, j), t2, (j, 2 * s if s else d),
+            {"y": y_at(sign)},
         )
 
     def tok_core(j, delta, receive):
@@ -200,36 +231,38 @@
                 tok_core(j, delta, True).wait_recv()
 
     token_plan = {
-        2: [(tokens_in, 0)], 3: [(tokens_in, 1), (tokens_in, 2)],
-        4: [(tokens_in, 3), (tokens_hop, 0)], 5: [(tokens_in, 4), (tokens_hop, 1)],
-        6: [(tokens_in, 5), (tokens_last, 0), (tokens_hop, 2)],
-        7: [(tokens_last, 1), (tokens_hop, 3)], 8: [(tokens_last, 2), (tokens_hop, 4)],
-        9: [(tokens_last, 3), (tokens_hop, 5)], 10: [(tokens_last, 4), (tokens_last, 5)],
+        2: [(tokens_in, 0)], 3: [(tokens_in, 1)],
+        4: [(tokens_in, 2), (tokens_hop, 0)], 5: [(tokens_in, 3), (tokens_hop, 1)],
+        6: [(tokens_in, 4), (tokens_last, 0), (tokens_hop, 2)],
+        7: [(tokens_in, 5), (tokens_last, 1), (tokens_hop, 3)],
+        8: [(tokens_last, 2), (tokens_hop, 4)], 9: [(tokens_last, 3), (tokens_hop, 5)],
+        10: [(tokens_last, 4)], 11: [(tokens_last, 5)],
     }
-    token_sends = {0: (0, 1), 1: (2,), 2: (3,), 3: (4,), 4: (5,)}
+    token_sends = {0: (0, 1, 2), 1: (3, 4), 2: (5,)}
+    lags = (2, 1, 0)
 
     def arrivals(step):
         return {0: (0,), 1: (1, 2), 2: (3, 4), 3: (5, 6), 4: (7,)}.get(step, ())
 
     def events(u, s):
-        lag = 1 if u < 2 else 0
+        lag = lags[u]
         if s == 0:
-            px_partner(u, mx).start()
-            px_mate(u, mx).start()
+            send(px_partner, u, mx)
+            send(px_mate, u, mx)
         if 1 <= s <= 4:
             for d in (0, 1):
-                for item in qz(u, d, s - 1, 1):
-                    item.wait_recv()
+                qz_mine(u, d, s - 1, 1).wait_recv()
+                qz_other(u, d, s - 1, 1).wait_recv()
         if s <= 3:
             for d in (0, 1):
-                for item in qz(u, d, s, 0):
-                    item.start()
+                send(qz_mine, u, d, s, 0)
+                send(qz_other, u, d, s, 0)
         for i in arrivals(s):
-            qx_partner(u, i, mx).start()
-            qx_mate(u, i, mx).start()
+            send(qx_partner, u, i, mx)
+            send(qx_mate, u, i, mx)
         if s == 1:
             px_partner(u, partner).wait_recv()
-            px_forward(u, partner).start()
+            send(px_forward, u, partner)
         for k in (0, 1):
             hop = s - 1 - k
             if hop == 0:
@@ -241,10 +274,10 @@
                 if 1 <= hop <= 3 or (hop == 4 and k == d):
                     pzc(u, d, hop - 1, k, 1).wait_recv()
                 if 0 <= hop <= 2 or (hop == 3 and k == d):
-                    pzc(u, d, hop, k, 0).start()
+                    send(pzc, u, d, hop, k, 0)
         for i in arrivals(s - 2 - lag):
             qx_partner(u, i, partner).wait_recv()
-            qx_forward(u, i, partner).start()
+            send(qx_forward, u, i, partner)
 
     def arrived(u, group_at):
         for i in arrivals(group_at):
@@ -258,32 +291,32 @@
             preferred_element_type=jnp.float32,
         )
 
-    def project(u, slots, group_at):
+    def project(u, slots, shift, group_at):
         if group_at == 0:
             for slot in slots:
-                acc[slot] = product(u, slot, mz)
+                acc[slot + shift] = product(u, slot, mz)
             return
         sides = len(arrivals(group_at))
 
         def step(index, carry):
             slot = index // sides if len(slots) == 2 else slots[0]
             sign = 1 - 2 * lax.rem(index, sides)
-            acc[slot] += product(u, slot, lax.rem(mz + sign * group_at + NZ, NZ))
+            acc[slot + shift] += product(u, slot, lax.rem(mz + sign * group_at + NZ, NZ))
             return carry
 
         lax.fori_loop(0, sides * len(slots), step, 0)
 
-    def project_all(u, slot):
-        acc[slot] = product(u, slot, 0)
+    def project_all(u, slot, shift):
+        acc[slot + shift] = product(u, slot, 0)
 
         def step(block, carry):
-            acc[slot] += product(u, slot, block)
+            acc[slot + shift] += product(u, slot, block)
             return carry
 
         lax.fori_loop(1, NZ, step, 0)
 
-    def activate(u, slot):
-        total = acc[slot]
+    def activate(u, slot, shift):
+        total = acc[slot + shift]
         act = (total / (1.0 + jnp.exp(-total))).astype(jnp.bfloat16)
         qkv[u, slot] = act
         if u < 2:
@@ -337,7 +370,7 @@
 
     for step in range(STEPS):
         for u in reversed(range(UNITS)):
-            if 0 <= step - 4 * u <= 7:
+            if 0 <= step - 4 * u <= 8:
                 events(u, step - 4 * u)
         for j in token_sends.get(step, ()):
             tok_x(j).start()
@@ -358,33 +391,31 @@
         if step == 4:
             tok_copy.wait()
         for u in (0, 1):
-            part = step - 4 * u - 4
+            part = step - 4 * u - 3 - lags[u]
             if 0 <= part <= 4:
                 arrived(u, part)
-                project(u, (0,), part)
+                project(u, (0,), u, part)
                 if part == 4:
-                    activate(u, 0)
+                    activate(u, 0, u)
         if step == 11:
             tokens_end()
-            project_all(0, 1)
-            activate(0, 1)
+            project_all(0, 1, 1)
+            activate(0, 1, 1)
         if step == 12:
-            project_all(1, 1)
-            activate(1, 1)
-            parts = (0, 1)
-        else:
-            parts = (step - 11,) if step > 12 else ()
+            project_all(1, 1, -1)
+            activate(1, 1, -1)
+        parts = {13: (0, 1), 14: (2, 3), 15: (4,)}.get(step, ())
         for part in parts:
             arrived(2, part)
-            project(2, (1, 0), part)
+            project(2, (1, 0), 1, part)
         if step == 13:
             for slot, place in ((0, mx), (1, partner)):
                 t4[place] = tails[mine, slot]
             row_tail()
         if step == 14:
             row_pair()
-    activate(2, 1)
-    activate(2, 0)
+    activate(2, 1, 1)
+    activate(2, 0, 1)
 
     def within(j, slot):
         for i in range(TILES):
@@ -460,11 +491,15 @@
     for k in range(1, PEERS):
         square_copy(0, k).start()
     gain = gain_ref[...].astype(jnp.float32)
+    is_first = (group == 0).astype(jnp.float32)
+
+    def gain_of(first):
+        rows = [gain[j:j + 1] * first + gain[2 + j:3 + j] * (1.0 - first) for j in (0, 1)]
+        return jnp.concatenate(rows, axis=1)
+
+    own_gain, other_gain = gain_of(is_first), gain_of(1.0 - is_first)
     own_columns = pl.ds(pl.multiple_of(group * WID, WID), WID)
     other_columns = pl.ds(pl.multiple_of((1 - group) * WID, WID), WID)
-    is_first = (group == 0).astype(jnp.float32)
-    own_gain = gain[:, :WID] * is_first + gain[:, WID:] * (1.0 - is_first)
-    other_gain = gain[:, WID:] * is_first + gain[:, :WID] * (1.0 - is_first)
     for side in (0, 1):
         for k in range(PEERS):
             if side or k:
@@ -492,21 +527,21 @@
         for a in (2 * i, 2 * i + 1):
             write(other_columns, orecv, other_gain, a)
 
-    for u in range(UNITS):
-        px_mate(u, mx).wait_send()
-        px_partner(u, mx).wait_send()
-        px_forward(u, partner).wait_send()
-        for d in (0, 1):
-            for s in range(4):
-                for item in qz(u, d, s, 0):
-                    item.wait_send()
-                for k in (0, 1):
-                    if s < 3 or k == d:
-                        pzc(u, d, s, k, 0).wait_send()
-        for i in range(NZ):
-            qx_mate(u, i, mx).wait_send()
-            qx_partner(u, i, mx).wait_send()
-            qx_forward(u, i, partner).wait_send()
+    last = UNITS - 1
+    px_mate(last, mx).wait_send()
+    px_partner(last, mx).wait_send()
+    px_forward(last, partner).wait_send()
+    for d in (0, 1):
+        for s in range(4):
+            qz_mine(last, d, s, 0).wait_send()
+            qz_other(last, d, s, 0).wait_send()
+            for k in (0, 1):
+                if s < 3 or k == d:
+                    pzc(last, d, s, k, 0).wait_send()
+    for i in range(NZ):
+        qx_mate(last, i, mx).wait_send()
+        qx_partner(last, i, mx).wait_send()
+        qx_forward(last, i, partner).wait_send()
     for j in range(SUBS):
         tok_x(j).wait_send()
         for d in (0, 1):
@@ -528,30 +563,30 @@
 
 
 def shards(tokens, w_query, w_keyval, doc_lengths, norm_gain):
-    halves = []
-    for g in (0, 1):
-        halves += [w_keyval[:, 2 * g + j, :] for j in (0, 1)]
-        halves.append(w_query[:, 2 * g:2 * g + 2, :].reshape(ROWS, WID))
-    w_in = jnp.stack(halves).reshape(2, UNITS, ROWS, WID)
+    w_kv = jnp.transpose(w_keyval, (1, 0, 2))
+    w_q = jnp.transpose(w_query, (1, 0, 2))
     vmem = pl.BlockSpec(memory_space=pltpu.VMEM)
     smem = pl.BlockSpec(memory_space=pltpu.SMEM)
     anywhere = pl.BlockSpec(memory_space=pl.ANY)
 
     def dma(*shape):
         return pltpu.SemaphoreType.DMA((2, *shape))
+
+    def units(*shape):
+        return pltpu.SemaphoreType.DMA((1 + UNITS, *shape))
 
     f32, bf16 = jnp.float32, jnp.bfloat16
     return pl.pallas_call(
         kernel,
         out_shape=jax.ShapeDtypeStruct((TOK, 2 * WID), bf16),
-        in_specs=[smem, anywhere, anywhere, vmem],
+        in_specs=[smem, anywhere, anywhere, anywhere, vmem],
         out_specs=vmem,
         scratch_shapes=[
             pltpu.VMEM((UNITS, NZ, NX, ROWS, WID), bf16),
             pltpu.VMEM((UNITS, NZ, QR, WID), bf16),
             pltpu.VMEM((UNITS, PR, WID), bf16),
             pltpu.VMEM((2, TOK, DM), bf16),
-            pltpu.VMEM((2, TOK, WID), f32),
+            pltpu.VMEM((3, TOK, WID), f32),
             pltpu.VMEM((UNITS, 2, TOK, WID), bf16),
             pltpu.VMEM((2, TOK, 1), jnp.int32),
             pltpu.VMEM((2, 2, DH, DH), f32),
@@ -564,18 +599,18 @@
             pltpu.VMEM((2, 8, DH), f32),
             pltpu.VMEM((TOK, WID), bf16),
             pltpu.VMEM((TOK, WID), bf16),
-            pltpu.SemaphoreType.DMA((4,)),
-            dma(UNITS), dma(UNITS), dma(UNITS),
-            dma(UNITS, 2, 4), dma(UNITS, 2, 4), dma(UNITS, 2, 4, 2),
-            dma(UNITS, NZ), dma(UNITS, NZ), dma(UNITS, NZ),
-            dma(SUBS), dma(SUBS, 2, 2), dma(SUBS, NY),
+            pltpu.SemaphoreType.DMA((10,)),
+            units(), units(), units(),
+            units(2, 4), units(2, 4), units(2, 4, 2),
+            units(NZ), units(NZ), units(NZ),
+            dma(SUBS), dma(SUBS, 3), dma(SUBS, NY),
             dma(2), dma(3), dma(2), dma(2, PEERS), dma(TILES),
         ],
         compiler_params=pltpu.CompilerParams(
             collective_id=0, has_side_effects=True, vmem_limit_bytes=62 << 20
         ),
         name="layer",
-    )(doc_lengths, tokens, w_in, norm_gain.reshape(1, 2 * WID))
+    )(doc_lengths, tokens, w_kv, w_q, norm_gain.reshape(4, DH))
 
 
 def solution(mesh):

time: 132 us -> 135 us (1.023)
  Pallas kernels: 125 us -> 130 us
  local copies, waits for them, and re-layouts: 7.07 us -> 5.47 us
    pallas_call x1, Pallas kernels: 125 us -> 130 us  [shards(): pl.pallas_call(kernel, out_shape=jax.ShapeDtypeStruct((TOK, 2 * WID), bf1...]
    slice x2 -> x0, local copies, waits for them, and re-layouts: 3.5 us -> none  [the longest x1 2.31 us: shards(): halves += [w_keyval[:, 2 * g + j, :] for j in (0, 1)]]
    unnamed x8 -> x3, local copies, waits for them, and re-layouts: 2.14 us -> 5.47 us
where the time goes in v4:
time: 135 us
  Pallas kernels  130 us (96%)
  local copies, waits for them, and re-layouts  5.47 us (4%)
    pallas_call x1, Pallas kernels, shards(): pl.pallas_call(kernel, out_shape=jax.ShapeDtypeStruct((TOK, 2 * WID), bf1...  130 us
    unnamed x3, local copies, waits for them, and re-layouts  5.47 us

profile of v4, /device:TPU:1, one launch (start us, length us, event | category | flops | bytes accessed | tf_op | source)
XLA Modules:
  0.0 135.2 jit_solution(8230299526105154363)
XLA Ops:
  0.0 1.6 %copy.11 = bf16[192,4,128]{2,0,1:T(8,128)(2,1)} copy(bf16[192,4,128]{2,1,0:T(4,128)(2,1)} %param.6) | data formatting | bytes 393216 | tf_op args[1]
  1.6 1.8 %copy.10 = bf16[192,4,256]{2,0,1:T(8,128)(2,1)} copy(bf16[192,4,256]{2,1,0:T(4,128)(2,1)} %param.7) | data formatting | bytes 786432 | tf_op args[2]
  3.4 129.7 %layer.1 = bf16[768,512]{1,0:T(8,128)(2,1)} custom-call(s32[8]{0:T(128)} %len_ref.1, bf16[768,6144]{1,0:T(8,128)(2,1)} %tok_hbm.1, bf16[4,192,256]{2,1,0:T(8,128)(2,1)} %bitcast.7, bf16[4,192,128]{2,1,0:T(8,128)(2,1)} %bitcast.8, bf16[4,128]{1,0:T(4,128)(2,1)} %bitcast.9), custom_call_target="tpu_custom_call" | custom-call | tf_op jit(solution)/shard_map/layer/pallas_call | solution.py:579
  133.2 2.1 %copy.13 = bf16[768,512]{1,0:T(8,128)(2,1)} copy(bf16[768,512]{1,0:T(8,128)(2,1)} %layer.1) | data formatting | bytes 1572864

commit v5 on v4

--- a/solution.py
+++ b/solution.py
@@ -16,9 +16,8 @@
 DM = 6144
 DH = 128
 PIECE = TOK // PEERS
-SUBS = 6
+SUBS = 3
 SUB = PIECE // SUBS
-STEPS = 16
 TILE = 256
 TILES = TOK // TILE
 MESH = pl.DeviceIdType.MESH
@@ -170,28 +169,25 @@
             pz, u, (d, s, k), {"z": z_at(sign)},
         )
 
-    def block_at(i):
-        if i == 0:
-            return mz
-        distance = (i + 1) // 2
-        return z_at(-distance if i % 2 else distance)
-
-    def lower(u, i, x):
-        return wbuf.at[u, block_at(i), x, pl.ds(PR, QR), :]
-
-    def qx_mate(u, i, x):
-        return unit_same(lower(u, i, x), qxm, u, (i,), to_mate)
-
-    def qx_partner(u, i, x):
+    def lower(u, k, x):
+        return wbuf.at[u, pl.ds(2 * k, 2), x, pl.ds(PR, QR), :]
+
+    def qx_mate(u, k, x):
+        return unit_same(lower(u, k, x), qxm, u, (k,), to_mate)
+
+    def qx_partner(u, k, x):
         return unit_copy(
-            tbuf.at[u, block_at(i)], lower(u, i, x), qxp, u, (i,), to_partner
+            tbuf.at[u, pl.ds(2 * k, 2)], lower(u, k, x), qxp, u, (k,), to_partner
         )
 
-    def qx_forward(u, i, x):
-        return unit_same(lower(u, i, x), qxf, u, (i,), to_mate)
-
-    def token_rows(y, core, j):
-        return tokv.at[1, pl.ds((y * NC + core) * PIECE + j * SUB, SUB), :]
+    def qx_forward(u, k, x):
+        return unit_same(lower(u, k, x), qxf, u, (k,), to_mate)
+
+    def token_rows(y, core, j, half=None):
+        start = (y * NC + core) * PIECE + j * SUB
+        if half is None:
+            return tokv.at[1, pl.ds(start, SUB), :]
+        return tokv.at[1, pl.ds(start + half * (SUB // 2), SUB // 2), :]
 
     def tok_x(j):
         start = me * PIECE + j * SUB
@@ -199,10 +195,8 @@
 
     def tok_y(j, d, s, lag):
         sign = 1 - 2 * d
-        return same(
-            token_rows(y_at(-sign * (s + lag)), mc, j), t2, (j, 2 * s if s else d),
-            {"y": y_at(sign)},
-        )
+        rows = token_rows(y_at(-sign * (s + lag)), mc, j, None if s == 0 else d)
+        return same(rows, t2, (j, d, s), {"y": y_at(sign)})
 
     def tok_core(j, delta, receive):
         core = 1 - mc if receive else mc
@@ -217,12 +211,13 @@
     def tokens_hop(j):
         for d in (0, 1):
             tok_y(j, d, 0, 1).wait_recv()
-        tok_y(j, j % 2, 1, 0).start()
+            tok_y(j, d, 1, 0).start()
         for delta in (1, -1):
             tok_core(j, delta, False).start()
 
     def tokens_last(j):
-        tok_y(j, j % 2, 1, 1).wait_recv()
+        for d in (0, 1):
+            tok_y(j, d, 1, 1).wait_recv()
         tok_core(j, 2, False).start()
 
     def tokens_end():
@@ -231,92 +226,75 @@
                 tok_core(j, delta, True).wait_recv()
 
     token_plan = {
-        2: [(tokens_in, 0)], 3: [(tokens_in, 1)],
-        4: [(tokens_in, 2), (tokens_hop, 0)], 5: [(tokens_in, 3), (tokens_hop, 1)],
-        6: [(tokens_in, 4), (tokens_last, 0), (tokens_hop, 2)],
-        7: [(tokens_in, 5), (tokens_last, 1), (tokens_hop, 3)],
-        8: [(tokens_last, 2), (tokens_hop, 4)], 9: [(tokens_last, 3), (tokens_hop, 5)],
-        10: [(tokens_last, 4)], 11: [(tokens_last, 5)],
+        3: [(tokens_in, 0)], 5: [(tokens_in, 1)], 6: [(tokens_hop, 0)],
+        7: [(tokens_hop, 1)], 8: [(tokens_in, 2), (tokens_last, 0)], 9: [(tokens_last, 1)],
+        11: [(tokens_hop, 2)], 12: [(tokens_last, 2)],
     }
-    token_sends = {0: (0, 1, 2), 1: (3, 4), 2: (5,)}
-    lags = (2, 1, 0)
-
-    def arrivals(step):
-        return {0: (0,), 1: (1, 2), 2: (3, 4), 3: (5, 6), 4: (7,)}.get(step, ())
-
-    def events(u, s):
-        lag = lags[u]
-        if s == 0:
-            send(px_partner, u, mx)
-            send(px_mate, u, mx)
-        if 1 <= s <= 4:
+
+    def phase1_start(n):
+        for d in (0, 1):
+            send(qz_mine, n, d, 0, 0)
+            send(qz_other, n, d, 0, 0)
+        send(px_partner, n, mx)
+        send(px_mate, n, mx)
+
+    def phase1_step(n, s):
+        for d in (0, 1):
+            qz_mine(n, d, s - 1, 1).wait_recv()
+            qz_other(n, d, s - 1, 1).wait_recv()
+            send(qz_mine, n, d, s, 0)
+            send(qz_other, n, d, s, 0)
+        if s == 1:
+            px_partner(n, partner).wait_recv()
+            send(px_forward, n, partner)
+
+    def phase2_start(p):
+        px_mate(p, mate).wait_recv()
+        px_forward(p, across).wait_recv()
+        for k in (0, 1):
             for d in (0, 1):
-                qz_mine(u, d, s - 1, 1).wait_recv()
-                qz_other(u, d, s - 1, 1).wait_recv()
-        if s <= 3:
+                send(pzc, p, d, 0, k, 0)
+        for d in (0, 1):
+            qz_mine(p, d, 3, 1).wait_recv()
+            qz_other(p, d, 3, 1).wait_recv()
+        for k in range(4):
+            send(qx_partner, p, k, mx)
+            send(qx_mate, p, k, mx)
+
+    def phase2_step(p, s):
+        for k in (0, 1):
             for d in (0, 1):
-                send(qz_mine, u, d, s, 0)
-                send(qz_other, u, d, s, 0)
-        for i in arrivals(s):
-            send(qx_partner, u, i, mx)
-            send(qx_mate, u, i, mx)
-        if s == 1:
-            px_partner(u, partner).wait_recv()
-            send(px_forward, u, partner)
-        for k in (0, 1):
-            hop = s - 1 - k
-            if hop == 0:
-                if k == 0:
-                    px_mate(u, mate).wait_recv()
-                else:
-                    px_forward(u, across).wait_recv()
-            for d in (0, 1):
-                if 1 <= hop <= 3 or (hop == 4 and k == d):
-                    pzc(u, d, hop - 1, k, 1).wait_recv()
-                if 0 <= hop <= 2 or (hop == 3 and k == d):
-                    send(pzc, u, d, hop, k, 0)
-        for i in arrivals(s - 2 - lag):
-            qx_partner(u, i, partner).wait_recv()
-            send(qx_forward, u, i, partner)
-
-    def arrived(u, group_at):
-        for i in arrivals(group_at):
-            qx_mate(u, i, mate).wait_recv()
-            qx_forward(u, i, across).wait_recv()
-
-    def product(u, slot, block):
-        columns = pl.ds(pl.multiple_of(block * (DM // NZ), DH), DM // NZ)
-        return jnp.dot(
-            tokv[slot, :, columns], wbuf[u, block].reshape(DM // NZ, WID),
-            preferred_element_type=jnp.float32,
-        )
-
-    def project(u, slots, shift, group_at):
-        if group_at == 0:
-            for slot in slots:
-                acc[slot + shift] = product(u, slot, mz)
-            return
-        sides = len(arrivals(group_at))
-
-        def step(index, carry):
-            slot = index // sides if len(slots) == 2 else slots[0]
-            sign = 1 - 2 * lax.rem(index, sides)
-            acc[slot + shift] += product(u, slot, lax.rem(mz + sign * group_at + NZ, NZ))
+                pzc(p, d, s - 1, k, 1).wait_recv()
+                if s < 3 or k == d:
+                    send(pzc, p, d, s, k, 0)
+        for k in ((0,), (1, 2), (3,))[s - 1]:
+            qx_partner(p, k, partner).wait_recv()
+            send(qx_forward, p, k, partner)
+
+    def phase2_end(p):
+        for d in (0, 1):
+            pzc(p, d, 3, d, 1).wait_recv()
+        for k in range(4):
+            qx_mate(p, k, mate).wait_recv()
+            qx_forward(p, k, across).wait_recv()
+
+    def project(u, slot, lo, hi):
+        if lo == 0:
+            acc[...] = jnp.zeros_like(acc)
+
+        def step(pair, carry):
+            columns = pl.ds(pl.multiple_of(pair * (DM // 4), 128), DM // 4)
+            acc[...] += jnp.dot(
+                tokv[slot, :, columns],
+                wbuf[u, pl.ds(2 * pair, 2)].reshape(DM // 4, WID),
+                preferred_element_type=jnp.float32,
+            )
             return carry
 
-        lax.fori_loop(0, sides * len(slots), step, 0)
-
-    def project_all(u, slot, shift):
-        acc[slot + shift] = product(u, slot, 0)
-
-        def step(block, carry):
-            acc[slot + shift] += product(u, slot, block)
-            return carry
-
-        lax.fori_loop(1, NZ, step, 0)
-
-    def activate(u, slot, shift):
-        total = acc[slot + shift]
+        lax.fori_loop(lo, hi, step, 0)
+
+    def activate(u, slot):
+        total = acc[...]
         act = (total / (1.0 + jnp.exp(-total))).astype(jnp.bfloat16)
         qkv[u, slot] = act
         if u < 2:
@@ -368,54 +346,52 @@
         kept = (mz >= 1) & (mz * (NX * TOK) - 1 >= row_last)
         rt[2] = rt[0] + kept.astype(jnp.float32) * rt[1]
 
-    for step in range(STEPS):
-        for u in reversed(range(UNITS)):
-            if 0 <= step - 4 * u <= 8:
-                events(u, step - 4 * u)
-        for j in token_sends.get(step, ()):
-            tok_x(j).start()
+    for step in range(16):
+        r, s = step // 4, step % 4
+        n, p, c = r, r - 1, r - 2
+        if s == 0:
+            if n < UNITS:
+                phase1_start(n)
+            if r == 0:
+                tok_x(0).start()
+                tok_x(1).start()
+                for slot in (0, 1):
+                    t = lax.broadcasted_iota(jnp.int32, (TOK, 1), 0) + bases[slot]
+                    starts[slot] = start_of(t, ends)
+            if p >= 0:
+                phase2_start(p)
+            if r == 1:
+                tok_x(2).start()
+            if c >= 0:
+                phase2_end(c)
+        else:
+            if n < UNITS:
+                phase1_step(n, s)
+            if p >= 0:
+                phase2_step(p, s)
         for action, j in token_plan.get(step, ()):
             action(j)
+        if r == 2:
+            if s == 0:
+                tok_copy.wait()
+            project(0, 0, s, s + 1)
+            if s == 3:
+                activate(0, 0)
+        if step == 12:
+            project(1, 0, 0, 4)
+            activate(1, 0)
         if step == 13:
+            tokens_end()
+            project(0, 1, 0, 4)
+            activate(0, 1)
+        if step == 14:
+            project(1, 1, 0, 4)
+            activate(1, 1)
+        if step == 15:
             tail_copy(0, mx).start()
             tail_copy(1, partner).start()
-        if step == 14:
-            relay(0).start()
-        if step == 15:
-            relay(1).start()
-            relay(2).start()
-        if step == 0:
-            for slot in (0, 1):
-                t = lax.broadcasted_iota(jnp.int32, (TOK, 1), 0) + bases[slot]
-                starts[slot] = start_of(t, ends)
-        if step == 4:
-            tok_copy.wait()
-        for u in (0, 1):
-            part = step - 4 * u - 3 - lags[u]
-            if 0 <= part <= 4:
-                arrived(u, part)
-                project(u, (0,), u, part)
-                if part == 4:
-                    activate(u, 0, u)
-        if step == 11:
-            tokens_end()
-            project_all(0, 1, 1)
-            activate(0, 1, 1)
-        if step == 12:
-            project_all(1, 1, -1)
-            activate(1, 1, -1)
-        parts = {13: (0, 1), 14: (2, 3), 15: (4,)}.get(step, ())
-        for part in parts:
-            arrived(2, part)
-            project(2, (1, 0), 1, part)
-        if step == 13:
             for slot, place in ((0, mx), (1, partner)):
                 t4[place] = tails[mine, slot]
-            row_tail()
-        if step == 14:
-            row_pair()
-    activate(2, 1, 1)
-    activate(2, 0, 1)
 
     def within(j, slot):
         for i in range(TILES):
@@ -432,6 +408,18 @@
                 weights, qkv[j, slot, 0:width, DH:2 * DH], preferred_element_type=jnp.float32
             )
 
+    phase2_end(2)
+    row_tail()
+    project(2, 1, 0, 2)
+    relay(0).start()
+    project(2, 1, 2, 4)
+    activate(2, 1)
+    project(2, 0, 0, 2)
+    row_pair()
+    project(2, 0, 2, 4)
+    relay(1).start()
+    relay(2).start()
+    activate(2, 0)
     for slot in (1, 0):
         within(0, slot)
         within(1, slot)
@@ -538,15 +526,15 @@
             for k in (0, 1):
                 if s < 3 or k == d:
                     pzc(last, d, s, k, 0).wait_send()
-    for i in range(NZ):
-        qx_mate(last, i, mx).wait_send()
-        qx_partner(last, i, mx).wait_send()
-        qx_forward(last, i, partner).wait_send()
+    for k in range(4):
+        qx_mate(last, k, mx).wait_send()
+        qx_partner(last, k, mx).wait_send()
+        qx_forward(last, k, partner).wait_send()
     for j in range(SUBS):
         tok_x(j).wait_send()
         for d in (0, 1):
             tok_y(j, d, 0, 0).wait_send()
-        tok_y(j, j % 2, 1, 0).wait_send()
+            tok_y(j, d, 1, 0).wait_send()
         for delta in (0, 1, -1, 2):
             tok_core(j, delta, False).wait_send()
     for slot in (0, 1):
@@ -586,7 +574,7 @@
             pltpu.VMEM((UNITS, NZ, QR, WID), bf16),
             pltpu.VMEM((UNITS, PR, WID), bf16),
             pltpu.VMEM((2, TOK, DM), bf16),
-            pltpu.VMEM((3, TOK, WID), f32),
+            pltpu.VMEM((TOK, WID), f32),
             pltpu.VMEM((UNITS, 2, TOK, WID), bf16),
             pltpu.VMEM((2, TOK, 1), jnp.int32),
             pltpu.VMEM((2, 2, DH, DH), f32),
@@ -602,8 +590,8 @@
             pltpu.SemaphoreType.DMA((10,)),
             units(), units(), units(),
             units(2, 4), units(2, 4), units(2, 4, 2),
-            units(NZ), units(NZ), units(NZ),
-            dma(SUBS), dma(SUBS, 3), dma(SUBS, NY),
+            units(4), units(4), units(4),
+            dma(SUBS), dma(SUBS, 2, 2), dma(SUBS, NY),
             dma(2), dma(3), dma(2), dma(2, PEERS), dma(TILES),
         ],
         compiler_params=pltpu.CompilerParams(

time: 135 us -> 125 us (0.926)
  Pallas kernels: 130 us -> 120 us
    pallas_call x1, Pallas kernels: 130 us -> 120 us  [shards(): pl.pallas_call(kernel, out_shape=jax.ShapeDtypeStruct((TOK, 2 * WID), bf1...]
where the time goes in v5:
time: 125 us
  Pallas kernels  120 us (96%)
  local copies, waits for them, and re-layouts  5.47 us (4%)
    pallas_call x1, Pallas kernels, shards(): pl.pallas_call(kernel, out_shape=jax.ShapeDtypeStruct((TOK, 2 * WID), bf1...  120 us
    unnamed x3, local copies, waits for them, and re-layouts  5.47 us

profile of v5, /device:TPU:1, one launch (start us, length us, event | category | flops | bytes accessed | tf_op | source)
XLA Modules:
  0.0 125.0 jit_solution(2749109992028732596)
XLA Ops:
  0.0 1.6 %copy.11 = bf16[192,4,128]{2,0,1:T(8,128)(2,1)} copy(bf16[192,4,128]{2,1,0:T(4,128)(2,1)} %param.6) | data formatting | bytes 393216 | tf_op args[1]
  1.6 1.8 %copy.10 = bf16[192,4,256]{2,0,1:T(8,128)(2,1)} copy(bf16[192,4,256]{2,1,0:T(4,128)(2,1)} %param.7) | data formatting | bytes 786432 | tf_op args[2]
  3.4 119.5 %layer.1 = bf16[768,512]{1,0:T(8,128)(2,1)} custom-call(s32[8]{0:T(128)} %len_ref.1, bf16[768,6144]{1,0:T(8,128)(2,1)} %tok_hbm.1, bf16[4,192,256]{2,1,0:T(8,128)(2,1)} %bitcast.7, bf16[4,192,128]{2,1,0:T(8,128)(2,1)} %bitcast.8, bf16[4,128]{1,0:T(4,128)(2,1)} %bitcast.9), custom_call_target="tpu_custom_call" | custom-call | tf_op jit(solution)/shard_map/layer/pallas_call | solution.py:567
  123.0 2.1 %copy.13 = bf16[768,512]{1,0:T(8,128)(2,1)} copy(bf16[768,512]{1,0:T(8,128)(2,1)} %layer.1) | data formatting | bytes 1572864

commit v6 on v5

--- a/solution.py
+++ b/solution.py
@@ -267,6 +267,9 @@
                 pzc(p, d, s - 1, k, 1).wait_recv()
                 if s < 3 or k == d:
                     send(pzc, p, d, s, k, 0)
+        if p == UNITS - 1 and s == 3:
+            tail_copy(0, mx).start()
+            tail_copy(1, partner).start()
         for k in ((0,), (1, 2), (3,))[s - 1]:
             qx_partner(p, k, partner).wait_recv()
             send(qx_forward, p, k, partner)
@@ -280,11 +283,11 @@
 
     def project(u, slot, lo, hi):
         if lo == 0:
-            acc[...] = jnp.zeros_like(acc)
+            acc[slot] = jnp.zeros((TOK, WID), jnp.float32)
 
         def step(pair, carry):
             columns = pl.ds(pl.multiple_of(pair * (DM // 4), 128), DM // 4)
-            acc[...] += jnp.dot(
+            acc[slot] += jnp.dot(
                 tokv[slot, :, columns],
                 wbuf[u, pl.ds(2 * pair, 2)].reshape(DM // 4, WID),
                 preferred_element_type=jnp.float32,
@@ -294,7 +297,7 @@
         lax.fori_loop(lo, hi, step, 0)
 
     def activate(u, slot):
-        total = acc[...]
+        total = acc[slot]
         act = (total / (1.0 + jnp.exp(-total))).astype(jnp.bfloat16)
         qkv[u, slot] = act
         if u < 2:
@@ -388,10 +391,9 @@
             project(1, 1, 0, 4)
             activate(1, 1)
         if step == 15:
-            tail_copy(0, mx).start()
-            tail_copy(1, partner).start()
             for slot, place in ((0, mx), (1, partner)):
                 t4[place] = tails[mine, slot]
+            row_tail()
 
     def within(j, slot):
         for i in range(TILES):
@@ -408,15 +410,17 @@
                 weights, qkv[j, slot, 0:width, DH:2 * DH], preferred_element_type=jnp.float32
             )
 
-    phase2_end(2)
-    row_tail()
-    project(2, 1, 0, 2)
-    relay(0).start()
-    project(2, 1, 2, 4)
+    for d in (0, 1):
+        pzc(2, d, 3, d, 1).wait_recv()
+    for k in range(4):
+        qx_mate(2, k, mate).wait_recv()
+        qx_forward(2, k, across).wait_recv()
+        for slot in (1, 0):
+            project(2, slot, k, k + 1)
+        if k == 0:
+            relay(0).start()
+    row_pair()
     activate(2, 1)
-    project(2, 0, 0, 2)
-    row_pair()
-    project(2, 0, 2, 4)
     relay(1).start()
     relay(2).start()
     activate(2, 0)
@@ -574,7 +578,7 @@
             pltpu.VMEM((UNITS, NZ, QR, WID), bf16),
             pltpu.VMEM((UNITS, PR, WID), bf16),
             pltpu.VMEM((2, TOK, DM), bf16),
-            pltpu.VMEM((TOK, WID), f32),
+            pltpu.VMEM((2, TOK, WID), f32),
             pltpu.VMEM((UNITS, 2, TOK, WID), bf16),
             pltpu.VMEM((2, TOK, 1), jnp.int32),
             pltpu.VMEM((2, 2, DH, DH), f32),

time: 125 us -> 123 us (0.984)
  Pallas kernels: 120 us -> 117 us
    pallas_call x1, Pallas kernels: 120 us -> 117 us  [shards(): pl.pallas_call(kernel, out_shape=jax.ShapeDtypeStruct((TOK, 2 * WID), bf1...]
where the time goes in v6:
time: 123 us
  Pallas kernels  117 us (95%)
  local copies, waits for them, and re-layouts  5.47 us (4%)
    pallas_call x1, Pallas kernels, shards(): pl.pallas_call(kernel, out_shape=jax.ShapeDtypeStruct((TOK, 2 * WID), bf1...  117 us
    unnamed x3, local copies, waits for them, and re-layouts  5.47 us

profile of v6, /device:TPU:1, one launch (start us, length us, event | category | flops | bytes accessed | tf_op | source)
XLA Modules:
  0.0 122.9 jit_solution(17330388818028428017)
XLA Ops:
  0.0 1.6 %copy.11 = bf16[192,4,128]{2,0,1:T(8,128)(2,1)} copy(bf16[192,4,128]{2,1,0:T(4,128)(2,1)} %param.6) | data formatting | bytes 393216 | tf_op args[1]
  1.6 1.8 %copy.10 = bf16[192,4,256]{2,0,1:T(8,128)(2,1)} copy(bf16[192,4,256]{2,1,0:T(4,128)(2,1)} %param.7) | data formatting | bytes 786432 | tf_op args[2]
  3.4 117.4 %layer.1 = bf16[768,512]{1,0:T(8,128)(2,1)} custom-call(s32[8]{0:T(128)} %len_ref.1, bf16[768,6144]{1,0:T(8,128)(2,1)} %tok_hbm.1, bf16[4,192,256]{2,1,0:T(8,128)(2,1)} %bitcast.7, bf16[4,192,128]{2,1,0:T(8,128)(2,1)} %bitcast.8, bf16[4,128]{1,0:T(4,128)(2,1)} %bitcast.9), custom_call_target="tpu_custom_call" | custom-call | tf_op jit(solution)/shard_map/layer/pallas_call | solution.py:571
  120.8 2.1 %copy.13 = bf16[768,512]{1,0:T(8,128)(2,1)} copy(bf16[768,512]{1,0:T(8,128)(2,1)} %layer.1) | data formatting | bytes 1572864
